TPU v7x, 256 devices: a whole 4x4x8 slice. The times are simulated.
256 devices in a mesh: fibre: 2 (over core), chan: 128 (over z, x, y).
Axes of the slice: x: 4, y: 4, z: 8, core: 2. Of those that a mesh axis runs over, the one named last changes fastest.
Arguments:
- raw: bfloat16 [32768, 4096], P(('fibre', 'chan'))
- starts: int32 [4], replicated, may hold values from 0 to 3072, as said below
- ref_ids: int32 [64], replicated, may hold values from 0 to 32767, as said below
- near_ids: int32 [32768, 8], P(('fibre', 'chan')), may hold values from 0 to 32767, as said below
- cross_ids: int32 [32768, 2], P(('fibre', 'chan')), may hold values from 0 to 255
- cross_mask: int32 [32768, 2], P(('fibre', 'chan')), may hold values 0 or 1
- export_loc: int32 [256], P(('fibre', 'chan')), may hold values from 0 to 127
Outputs:
- correlations: bfloat16 [32768, 64, 512], P(('fibre', 'chan'))
Inputs may be any that keep to these rules, and one draw needn't show every extreme that they name: starts[3] is 3072. `ref_ids`: distinct channel ids. `near_ids`: each neighbour lies on the same route as its channel (route = id // 16384) and at most 16 channels away from it.
All inputs are finite; a program needn't handle non-finite values. No bound on the sum of `cross_mask` on one device may be relied on, other than what follows from the above.
Results may differ from a plain program's by a relative error of at most 0.0063.
The roundings to bfloat16 on the way count: a program that leaves them out, or rounds other values in their place, can miss the bound.
Values may be sent and summed in bfloat16 or wider, within the bound.
A program may use at most 128 MiB of HBM per device.

v0:
```python
import math

import jax
import jax.numpy as jnp
from jax import lax
from jax.sharding import PartitionSpec as P

SEG = 1024
SEGS = 4
REFS = 64
LAGS = 512
NN = 8
HALO = 16


def with_halo(block, sides, width):
    for axis, dim in sides:
        count = lax.axis_size(axis)
        forward = [(i, i + 1) for i in range(count - 1)]
        backward = [(target, source) for source, target in forward]
        low = lax.ppermute(
            lax.slice_in_dim(block, block.shape[dim] - width, None, axis=dim), axis, forward
        )
        high = lax.ppermute(lax.slice_in_dim(block, 0, width, axis=dim), axis, backward)
        block = jnp.concatenate([low, block, high], axis=dim)
    return block


def forward_table():
    nbins = SEG // 2
    sample = jnp.arange(SEG, dtype=jnp.int32)
    freq = jnp.arange(nbins, dtype=jnp.int32)
    phase = jnp.mod(sample[:, None] * freq[None, :], SEG).astype(jnp.float32)
    theta = phase * (2.0 * math.pi / SEG)
    keep = (freq > 0).astype(jnp.float32)[None, :]
    return jnp.concatenate([jnp.cos(theta) * keep, -jnp.sin(theta)], 1).astype(jnp.bfloat16)


def lag_table():
    nbins = SEG // 2
    freq = jnp.arange(nbins, dtype=jnp.int32)
    lag = jnp.arange(LAGS, dtype=jnp.int32) - LAGS // 2
    phase = jnp.mod(freq[:, None] * lag[None, :], SEG).astype(jnp.float32)
    theta = phase * (2.0 * math.pi / SEG)
    scale = 1.0 / math.sqrt(nbins)
    table = jnp.concatenate([jnp.cos(theta) * scale, -jnp.sin(theta) * scale], 0)
    return table.astype(jnp.bfloat16)


def per_device(raw, starts, ref_ids, near_ids, cross_ids, cross_mask, export_loc):
    nbins = SEG // 2
    width = SEGS * SEG
    local_ch = raw.shape[0]
    block_base = lax.axis_index(("fibre", "chan")) * local_ch
    pieces = [lax.dynamic_slice_in_dim(raw, starts[s], SEG, 1) for s in range(SEGS)]
    segment = jnp.stack(pieces, 1)
    spectrum = jnp.dot(
        segment.reshape(local_ch * SEGS, SEG), forward_table(), preferred_element_type=jnp.float32
    )
    power = jnp.sum(spectrum * spectrum, -1, keepdims=True) / nbins
    whitened = (spectrum / jnp.sqrt(power + 1e-06)).astype(jnp.bfloat16)
    flat = whitened.reshape(local_ch, width)
    columns = jnp.arange(local_ch, dtype=jnp.int32)
    pick = (ref_ids[:, None] - block_base == columns[None, :]).astype(jnp.bfloat16)
    selected = jnp.dot(pick, flat, preferred_element_type=jnp.float32)
    references = lax.psum(selected, ("fibre", "chan")).astype(jnp.bfloat16)
    extended = with_halo(flat, (("chan", 0),), HALO)
    ext_rows = local_ch + 2 * HALO
    position = near_ids - (block_base - HALO)
    near_count = jnp.sum(
        (position[:, :, None] == jnp.arange(ext_rows, dtype=jnp.int32)[None, None, :]).astype(
            jnp.float32
        ),
        1,
    )
    total = flat.astype(jnp.float32) + jnp.dot(
        near_count.astype(jnp.bfloat16), extended, preferred_element_type=jnp.float32
    )
    exported = jnp.take(flat, export_loc, axis=0)
    live = cross_mask == 1
    piece = lax.all_gather(exported, ("fibre", "chan"), axis=0, tiled=True)
    slots = jnp.arange(piece.shape[0], dtype=jnp.int32)
    hits = (cross_ids[:, :, None] == slots[None, None, :]) & live[:, :, None]
    weights = jnp.sum(hits.astype(jnp.float32), 1).astype(jnp.bfloat16)
    crossing = jnp.dot(weights, piece, preferred_element_type=jnp.float32)
    count = 1.0 + NN + jnp.sum(cross_mask.astype(jnp.float32), 1)
    smoothed = ((total + crossing) / count[:, None]).astype(jnp.bfloat16)
    kernel = lag_table()
    ref_split = references.reshape(REFS, SEGS, SEG)
    ref_re = ref_split[..., :nbins]
    ref_im = ref_split[..., nbins:]
    group = math.gcd(local_ch, 32)

    def correlate(rows):
        a_re = rows[..., :nbins]
        a_im = rows[..., nbins:]
        g_re = jnp.einsum(
            "csf,rsf->crf", a_re, ref_re, preferred_element_type=jnp.float32
        ) + jnp.einsum("csf,rsf->crf", a_im, ref_im, preferred_element_type=jnp.float32)
        g_im = jnp.einsum(
            "csf,rsf->crf", a_im, ref_re, preferred_element_type=jnp.float32
        ) - jnp.einsum("csf,rsf->crf", a_re, ref_im, preferred_element_type=jnp.float32)
        cross = (jnp.concatenate([g_re, g_im], -1) / SEGS).astype(jnp.bfloat16)
        out = jnp.dot(cross.reshape(group * REFS, SEG), kernel, preferred_element_type=jnp.float32)
        return out.astype(jnp.bfloat16).reshape(group, REFS, LAGS)

    result = lax.map(correlate, smoothed.reshape(local_ch // group, group, SEGS, SEG))
    return result.reshape(local_ch, REFS, LAGS)


def solution(mesh):
    in_specs = (
        P(("fibre", "chan"), None),
        P(),
        P(),
        P(("fibre", "chan"), None),
        P(("fibre", "chan"), None),
        P(("fibre", "chan"), None),
        P(("fibre", "chan")),
    )
    out_specs = P(("fibre", "chan"), None, None)
    return jax.shard_map(
        per_device, mesh=mesh, in_specs=in_specs, out_specs=out_specs, check_vma=False
    )
```

profile of v0, /device:TPU:1, one launch (start us, length us, event | category | flops | bytes accessed | tf_op | source)
XLA Modules:
  0.0 315.5 jit_solution(655089644088672558)
XLA Ops:
  6.5 1.5 fusion.53
  13.1 8.0 %negate_convert_fusion = bf16[1024,512]{1,0:T(8,128)(2,1)S(1)} fusion(), kind=kLoop, calls=%fused_computation.36 | loop fusion | flops 8388608 | bytes 1048576 | tf_op jit(solution)/shard_map/convert.3
  23.6 1.9 dynamic-slice_bitcast_fusion.3
  25.6 0.8 copy.42
  26.4 0.3 reshape.58
  26.7 7.9 %multiply_convert_fusion = bf16[1024,512]{1,0:T(8,128)(2,1)S(1)} fusion(f32[512]{0:T(512)S(1)} %fusion.48), kind=kLoop, calls=%fused_computation.37 | loop fusion | flops 8388608 | bytes 1050624 | tf_op jit(solution)/shard_map/convert.2
  34.6 1.3 multiply_reduce_fusion
  36.0 0.3 divide_convert_fusion
  36.3 0.7 reshape.59
  37.7 0.6 fusion.46
  38.4 4.0 %collective-permute-start = (bf16[16,4096]{1,0:T(8,128)(2,1)S(1)}, bf16[16,4096]{1,0:T(8,128)(2,1)S(1)}, u32[]{:S(2)}, u32[]{:S(2)}) collective-permute-start(bf16[16,4096]{1,0:T(8,128)(2,1)S(1)} %slice.41), channel_id=1, source_target_pairs={{0,1},{1,2},{2,3},{3,4},{4,5},{5,6},{6,7},{7,8},{8,9},{9,10},{10,1... | collective-permute-start | bytes 393224 | tf_op jit(solution)/shard_map/ppermute | solution.py:21
  42.6 1.3 collective-permute-start.1
  43.9 0.3 fusion.45
  44.3 88.9 %all-reduce.1 = bf16[64,4096]{1,0:T(8,128)(2,1)S(1)} all-reduce(f32[64,4096]{1,0:T(8,128)S(1)} %fusion.45), channel_id=1, replica_groups=mesh['fibre'=2,'chan'=128] {'fibre','chan'}, use_global_device_ids=true, to_apply=%region_4.5 | all-reduce | flops 262144 | bytes 1572864 | tf_op jit(solution)/shard_map/psum | solution.py:66
  133.2 0.4 reshape.61
  133.8 1.1 copy.48
  134.9 1.1 copy.49
  136.3 4.5 %multiply_convert_fusion.2 = (bf16[512,512]{1,0:T(8,128)(2,1)S(1)}, bf16[512,512]{1,0:T(8,128)(2,1)S(1)}) fusion(s32[512]{0:T(512)S(1)} %iota_add_fusion), kind=kLoop, calls=%fused_computation.55 | loop fusion | flops 4980736 | bytes 1050624 | tf_op jit(solution)/shard_map/convert
  140.8 1.0 pad_maximum_fusion.1
  141.8 16.6 %all-gather.3.cloned.1.call-done = bf16[256,1,4096]{2,1,0:T(2,128)(2,1)} async-done(((bf16[1,1,4096]{2,1,0:T(2,128)(2,1)}), bf16[256,1,4096]{2,1,0:T(2,128)(2,1)}) %all-gather.3.cloned.1.call-update) | async-done | bytes 2097168 | tf_op jit(solution)/shard_map/all_gather | solution.py:81
  158.4 4.7 %fusion.25 = f32[128,4096]{1,0:T(8,128)S(1)} fusion(bf16[256,1,4096]{2,1,0:T(2,128)(2,1)} %all-gather.3.cloned.1.call-done, bf16[128,256]{1,0:T(8,128)(2,1)S(1)} %convert_reduce_fusion.1), kind=kOutput, calls=%fused_computation.31 | convolution fusion | flops 268435456 | bytes 4259840 | tf_op jit(solution)/shard_map/dot_general | solution.py:85
  163.1 0.6 fusion.17
  163.8 0.8 reshape.60
  164.8 143.8 %while.11 = (s32[]{:T(128)}, bf16[4,32,64,512]{3,2,1,0:T(8,128)(2,1)}, bf16[4,32,4,1024]{3,2,1,0:T(4,128)(2,1)S(1)}, bf16[64,4,512]{0,1,2:T(4,128)(2,1)S(1)}, bf...) while((s32[]{:T(128)}, ...), condition=%wide.region_6.7_spmd, body=%wide.region_5.6_spmd.sunk | while | flops 2190475264 | bytes 77595424 | solution.py:107
  164.9 1.0 copy-done
  166.0 0.8 copy.57
  166.8 1.3 fusion.87
  168.1 4.9 %add_bitcast_fusion.2 = f32[32,64,512]{1,0,2:T(8,128)} fusion(f32[512,32,64]{2,1,0:T(8,128)S(1)} %fusion.87, bf16[64,4,512]{0,1,2:T(4,128)(2,1)S(1)} %copy-done.6, bf16[1,32,4,1024]{1,2,3,0:T(4,128)(2,1)S(1)} %copy.57), kind=kOutput, calls=%fused_computation.3.clone.1 | convolution fusion | flops 9437184 | bytes 8912896 | tf_op jit(solution)/shard_map/while/body/eval_jaxpr/csf,rsf->crf/dot_general | solution.py:99
  173.0 6.9 %copy.59 = f32[32,64,512]{2,1,0:T(8,128)} copy(f32[32,64,512]{1,0,2:T(8,128)} %add_bitcast_fusion.2) | data formatting | bytes 8388608 | tf_op jit(solution)/shard_map/while/body/eval_jaxpr/add | solution.py:97
  179.9 1.3 fusion.86
  181.3 4.9 %subtract_bitcast_fusion.2 = f32[32,64,512]{1,0,2:T(8,128)} fusion(f32[512,32,64]{2,1,0:T(8,128)S(1)} %fusion.86, bf16[64,4,512]{0,1,2:T(4,128)(2,1)S(1)} %copy-done.7, bf16[1,32,4,1024]{1,2,3,0:T(4,128)(2,1)S(1)} %copy.57), kind=kOutput, calls=%fused_computation.2.clone.1 | convolution fusion | flops 9437184 | bytes 8912896 | tf_op jit(solution)/shard_map/while/body/eval_jaxpr/csf,rsf->crf/dot_general | solution.py:102
  186.2 6.9 %copy.58 = f32[32,64,512]{2,1,0:T(8,128)} copy(f32[32,64,512]{1,0,2:T(8,128)} %subtract_bitcast_fusion.2) | data formatting | bytes 8388608 | tf_op jit(solution)/shard_map/while/body/eval_jaxpr/sub | solution.py:100
  193.1 5.8 %fusion.88 = bf16[2048,512]{1,0:T(8,128)(2,1)S(1)} fusion(bf16[1024,512]{1,0:T(8,128)(2,1)S(1)} %copy-done.2, f32[2048,512]{1,0:T(8,128)} %bitcast.74, f32[2048,512]{1,0:T(8,128)} %bitcast.73), kind=kOutput, calls=%fused_computation.6.clone.1 | convolution fusion | flops 2154823680 | bytes 11534336 | tf_op jit(solution)/shard_map/while/body/eval_jaxpr/dot_general | solution.py:104
  199.0 1.6 constant_dynamic-update-slice_fusion.2
  200.8 1.0 copy-done
  201.9 0.8 copy.57
  202.7 1.3 fusion.87
  204.0 4.9 %add_bitcast_fusion.2 = f32[32,64,512]{1,0,2:T(8,128)} fusion(f32[512,32,64]{2,1,0:T(8,128)S(1)} %fusion.87, bf16[64,4,512]{0,1,2:T(4,128)(2,1)S(1)} %copy-done.6, bf16[1,32,4,1024]{1,2,3,0:T(4,128)(2,1)S(1)} %copy.57), kind=kOutput, calls=%fused_computation.3.clone.1 | convolution fusion | flops 9437184 | bytes 8912896 | tf_op jit(solution)/shard_map/while/body/eval_jaxpr/csf,rsf->crf/dot_general | solution.py:99
  209.0 6.9 %copy.59 = f32[32,64,512]{2,1,0:T(8,128)} copy(f32[32,64,512]{1,0,2:T(8,128)} %add_bitcast_fusion.2) | data formatting | bytes 8388608 | tf_op jit(solution)/shard_map/while/body/eval_jaxpr/add | solution.py:97
  215.9 1.3 fusion.86
  217.2 4.9 %subtract_bitcast_fusion.2 = f32[32,64,512]{1,0,2:T(8,128)} fusion(f32[512,32,64]{2,1,0:T(8,128)S(1)} %fusion.86, bf16[64,4,512]{0,1,2:T(4,128)(2,1)S(1)} %copy-done.7, bf16[1,32,4,1024]{1,2,3,0:T(4,128)(2,1)S(1)} %copy.57), kind=kOutput, calls=%fused_computation.2.clone.1 | convolution fusion | flops 9437184 | bytes 8912896 | tf_op jit(solution)/shard_map/while/body/eval_jaxpr/csf,rsf->crf/dot_general | solution.py:102
  222.2 6.9 %copy.58 = f32[32,64,512]{2,1,0:T(8,128)} copy(f32[32,64,512]{1,0,2:T(8,128)} %subtract_bitcast_fusion.2) | data formatting | bytes 8388608 | tf_op jit(solution)/shard_map/while/body/eval_jaxpr/sub | solution.py:100
  229.1 5.8 %fusion.88 = bf16[2048,512]{1,0:T(8,128)(2,1)S(1)} fusion(bf16[1024,512]{1,0:T(8,128)(2,1)S(1)} %copy-done.2, f32[2048,512]{1,0:T(8,128)} %bitcast.74, f32[2048,512]{1,0:T(8,128)} %bitcast.73), kind=kOutput, calls=%fused_computation.6.clone.1 | convolution fusion | flops 2154823680 | bytes 11534336 | tf_op jit(solution)/shard_map/while/body/eval_jaxpr/dot_general | solution.py:104
  234.9 1.6 constant_dynamic-update-slice_fusion.2
  236.8 1.0 copy-done
  237.9 0.8 copy.57
  238.7 1.3 fusion.87
  240.0 4.9 %add_bitcast_fusion.2 = f32[32,64,512]{1,0,2:T(8,128)} fusion(f32[512,32,64]{2,1,0:T(8,128)S(1)} %fusion.87, bf16[64,4,512]{0,1,2:T(4,128)(2,1)S(1)} %copy-done.6, bf16[1,32,4,1024]{1,2,3,0:T(4,128)(2,1)S(1)} %copy.57), kind=kOutput, calls=%fused_computation.3.clone.1 | convolution fusion | flops 9437184 | bytes 8912896 | tf_op jit(solution)/shard_map/while/body/eval_jaxpr/csf,rsf->crf/dot_general | solution.py:99
  244.9 6.9 %copy.59 = f32[32,64,512]{2,1,0:T(8,128)} copy(f32[32,64,512]{1,0,2:T(8,128)} %add_bitcast_fusion.2) | data formatting | bytes 8388608 | tf_op jit(solution)/shard_map/while/body/eval_jaxpr/add | solution.py:97
  251.8 1.3 fusion.86
  253.2 4.9 %subtract_bitcast_fusion.2 = f32[32,64,512]{1,0,2:T(8,128)} fusion(f32[512,32,64]{2,1,0:T(8,128)S(1)} %fusion.86, bf16[64,4,512]{0,1,2:T(4,128)(2,1)S(1)} %copy-done.7, bf16[1,32,4,1024]{1,2,3,0:T(4,128)(2,1)S(1)} %copy.57), kind=kOutput, calls=%fused_computation.2.clone.1 | convolution fusion | flops 9437184 | bytes 8912896 | tf_op jit(solution)/shard_map/while/body/eval_jaxpr/csf,rsf->crf/dot_general | solution.py:102
  258.1 6.9 %copy.58 = f32[32,64,512]{2,1,0:T(8,128)} copy(f32[32,64,512]{1,0,2:T(8,128)} %subtract_bitcast_fusion.2) | data formatting | bytes 8388608 | tf_op jit(solution)/shard_map/while/body/eval_jaxpr/sub | solution.py:100
  265.0 5.8 %fusion.88 = bf16[2048,512]{1,0:T(8,128)(2,1)S(1)} fusion(bf16[1024,512]{1,0:T(8,128)(2,1)S(1)} %copy-done.2, f32[2048,512]{1,0:T(8,128)} %bitcast.74, f32[2048,512]{1,0:T(8,128)} %bitcast.73), kind=kOutput, calls=%fused_computation.6.clone.1 | convolution fusion | flops 2154823680 | bytes 11534336 | tf_op jit(solution)/shard_map/while/body/eval_jaxpr/dot_general | solution.py:104
  270.9 1.6 constant_dynamic-update-slice_fusion.2
  272.7 1.0 copy-done
  273.8 0.8 copy.57
  274.6 1.3 fusion.87
  275.9 4.9 %add_bitcast_fusion.2 = f32[32,64,512]{1,0,2:T(8,128)} fusion(f32[512,32,64]{2,1,0:T(8,128)S(1)} %fusion.87, bf16[64,4,512]{0,1,2:T(4,128)(2,1)S(1)} %copy-done.6, bf16[1,32,4,1024]{1,2,3,0:T(4,128)(2,1)S(1)} %copy.57), kind=kOutput, calls=%fused_computation.3.clone.1 | convolution fusion | flops 9437184 | bytes 8912896 | tf_op jit(solution)/shard_map/while/body/eval_jaxpr/csf,rsf->crf/dot_general | solution.py:99
  280.9 6.9 %copy.59 = f32[32,64,512]{2,1,0:T(8,128)} copy(f32[32,64,512]{1,0,2:T(8,128)} %add_bitcast_fusion.2) | data formatting | bytes 8388608 | tf_op jit(solution)/shard_map/while/body/eval_jaxpr/add | solution.py:97
  287.8 1.3 fusion.86
  289.1 4.9 %subtract_bitcast_fusion.2 = f32[32,64,512]{1,0,2:T(8,128)} fusion(f32[512,32,64]{2,1,0:T(8,128)S(1)} %fusion.86, bf16[64,4,512]{0,1,2:T(4,128)(2,1)S(1)} %copy-done.7, bf16[1,32,4,1024]{1,2,3,0:T(4,128)(2,1)S(1)} %copy.57), kind=kOutput, calls=%fused_computation.2.clone.1 | convolution fusion | flops 9437184 | bytes 8912896 | tf_op jit(solution)/shard_map/while/body/eval_jaxpr/csf,rsf->crf/dot_general | solution.py:102
  294.1 6.9 %copy.58 = f32[32,64,512]{2,1,0:T(8,128)} copy(f32[32,64,512]{1,0,2:T(8,128)} %subtract_bitcast_fusion.2) | data formatting | bytes 8388608 | tf_op jit(solution)/shard_map/while/body/eval_jaxpr/sub | solution.py:100
  301.0 5.8 %fusion.88 = bf16[2048,512]{1,0:T(8,128)(2,1)S(1)} fusion(bf16[1024,512]{1,0:T(8,128)(2,1)S(1)} %copy-done.2, f32[2048,512]{1,0:T(8,128)} %bitcast.74, f32[2048,512]{1,0:T(8,128)} %bitcast.73), kind=kOutput, calls=%fused_computation.6.clone.1 | convolution fusion | flops 2154823680 | bytes 11534336 | tf_op jit(solution)/shard_map/while/body/eval_jaxpr/dot_general | solution.py:104
  306.8 1.6 constant_dynamic-update-slice_fusion.2
  (86 shorter events, 2.6 us)
Async XLA Ops:
  6.5 151.9 %all-gather.3.cloned.1.call-start = ((), (), s32[]{:S(2)}) async-start(), calls=%async_computation | async-start | bytes 4210688 | tf_op jit(solution)/shard_map/all_gather | solution.py:81
  36.3 7.6 %copy-start.11 = (s32[64]{0:T(128)S(1)}, s32[64]{0:T(128)}, u32[]{:S(2)}) copy-start(s32[64]{0:T(128)} %param.11) | copy-start | bytes 772
  38.4 124.7 %collective-permute-start = (bf16[16,4096]{1,0:T(8,128)(2,1)S(1)}, bf16[16,4096]{1,0:T(8,128)(2,1)S(1)}, u32[]{:S(2)}, u32[]{:S(2)}) collective-permute-start(bf16[16,4096]{1,0:T(8,128)(2,1)S(1)} %slice.41), channel_id=1, source_target_pairs={{0,1},{1,2},{2,3},{3,4},{4,5},{5,6},{6,7},{7,8},{8,9},{9,10},{10,1... | collective-permute-start | bytes 393224 | tf_op jit(solution)/shard_map/ppermute | solution.py:21
  42.6 120.6 %collective-permute-start.1 = (bf16[16,4096]{1,0:T(8,128)(2,1)S(1)}, bf16[16,4096]{1,0:T(8,128)(2,1)S(1)}, u32[]{:S(2)}, u32[]{:S(2)}) collective-permute-start(bf16[16,4096]{1,0:T(8,128)(2,1)S(1)} %slice.43), channel_id=1, source_target_pairs={{1,0},{2,1},{3,2},{4,3},{5,4},{6,5},{7,6},{8,7},{9,8},{10,9},{11,1... | collective-permute-start | bytes 393224 | tf_op jit(solution)/shard_map/ppermute | solution.py:24
  133.1 2.9 copy-start.10
  133.2 2.9 copy-start.9
  133.2 3.0 copy-start.8
  163.8 1.0 copy-start.3
  164.8 1.0 copy-start
  166.7 1.3 copy-start.6
  173.0 6.9 %copy-start.4 = (bf16[64,4,512]{0,1,2:T(4,128)(2,1)S(1)}, bf16[64,4,512]{0,1,2:T(4,128)(2,1)}, u32[]{:S(2)}) copy-start(bf16[64,4,512]{0,1,2:T(4,128)(2,1)} %get-tuple-element.174) | copy-start | bytes 786436 | tf_op jit(solution)/shard_map/while
  179.9 1.3 copy-start.7
  186.2 6.9 %copy-start.2 = (bf16[1024,512]{1,0:T(8,128)(2,1)S(1)}, bf16[1024,512]{1,0:T(8,128)(2,1)}, u32[]{:S(2)}) copy-start(bf16[1024,512]{1,0:T(8,128)(2,1)} %get-tuple-element.163) | copy-start | bytes 3145732 | tf_op jit(solution)/shard_map/while
  198.9 1.6 copy-start.1
  199.0 1.8 copy-start.5
  200.8 1.0 copy-start
  202.7 1.3 copy-start.6
  209.0 6.9 %copy-start.4 = (bf16[64,4,512]{0,1,2:T(4,128)(2,1)S(1)}, bf16[64,4,512]{0,1,2:T(4,128)(2,1)}, u32[]{:S(2)}) copy-start(bf16[64,4,512]{0,1,2:T(4,128)(2,1)} %get-tuple-element.174) | copy-start | bytes 786436 | tf_op jit(solution)/shard_map/while
  215.9 1.3 copy-start.7
  222.2 6.9 %copy-start.2 = (bf16[1024,512]{1,0:T(8,128)(2,1)S(1)}, bf16[1024,512]{1,0:T(8,128)(2,1)}, u32[]{:S(2)}) copy-start(bf16[1024,512]{1,0:T(8,128)(2,1)} %get-tuple-element.163) | copy-start | bytes 3145732 | tf_op jit(solution)/shard_map/while
  234.9 1.6 copy-start.1
  234.9 1.8 copy-start.5
  236.8 1.0 copy-start
  238.7 1.3 copy-start.6
  244.9 6.9 %copy-start.4 = (bf16[64,4,512]{0,1,2:T(4,128)(2,1)S(1)}, bf16[64,4,512]{0,1,2:T(4,128)(2,1)}, u32[]{:S(2)}) copy-start(bf16[64,4,512]{0,1,2:T(4,128)(2,1)} %get-tuple-element.174) | copy-start | bytes 786436 | tf_op jit(solution)/shard_map/while
  251.8 1.3 copy-start.7
  258.1 6.9 %copy-start.2 = (bf16[1024,512]{1,0:T(8,128)(2,1)S(1)}, bf16[1024,512]{1,0:T(8,128)(2,1)}, u32[]{:S(2)}) copy-start(bf16[1024,512]{1,0:T(8,128)(2,1)} %get-tuple-element.163) | copy-start | bytes 3145732 | tf_op jit(solution)/shard_map/while
  270.8 1.6 copy-start.1
  270.9 1.8 copy-start.5
  272.7 1.0 copy-start
  274.6 1.3 copy-start.6
  280.9 6.9 %copy-start.4 = (bf16[64,4,512]{0,1,2:T(4,128)(2,1)S(1)}, bf16[64,4,512]{0,1,2:T(4,128)(2,1)}, u32[]{:S(2)}) copy-start(bf16[64,4,512]{0,1,2:T(4,128)(2,1)} %get-tuple-element.174) | copy-start | bytes 786436 | tf_op jit(solution)/shard_map/while
  287.8 1.3 copy-start.7
  294.1 6.9 %copy-start.2 = (bf16[1024,512]{1,0:T(8,128)(2,1)S(1)}, bf16[1024,512]{1,0:T(8,128)(2,1)}, u32[]{:S(2)}) copy-start(bf16[1024,512]{1,0:T(8,128)(2,1)} %get-tuple-element.163) | copy-start | bytes 3145732 | tf_op jit(solution)/shard_map/while
  306.8 1.6 copy-start.1
  306.8 1.8 copy-start.5
Sparse Core Ops, SparseCore 0:
  38.4 119.9 all-gather.2
where the time goes:
time: 316 us; the launch traced here: 315 us
  blocking collectives  88.9 us (28%)
  matrix products  80.2 us (25%)
  local copies, waits for them, and re-layouts  79.5 us (25%)
  other arithmetic  22.8 us (7%)
  between operations  21.9 us (7%)
  waiting for transfers between devices  16.6 us (5%)
  starting transfers between devices  5.32 us (2%)
    psum x1, blocking collectives, per_device(): references = lax.psum(selected, ('fibre', 'chan')).astype(jnp.bfloat16)  88.9 us
    add x4, local copies, waits for them, and re-layouts, correlate(): jnp.einsum('csf,rsf->crf', a_re, ref_re, preferred_element_type=jnp.float32)  27.7 us
    sub x4, local copies, waits for them, and re-layouts, correlate(): jnp.einsum('csf,rsf->crf', a_im, ref_re, preferred_element_type=jnp.float32)  27.7 us
    dot_general x4, matrix products, correlate(): jnp.dot(cross.reshape(group * REFS, SEG), kernel, preferred_element_type=...  23.2 us
    another operation x3, other arithmetic  20.4 us
    dot_general x4, matrix products, correlate(): jnp.einsum('csf,rsf->crf', a_re, ref_im, preferred_element_type=jnp.float32)  19.8 us
    dot_general x4, matrix products, correlate(): jnp.einsum('csf,rsf->crf', a_im, ref_im, preferred_element_type=jnp.float32)  19.8 us
    all_gather x1, waiting for transfers between devices, per_device(): piece = lax.all_gather(exported, ('fibre', 'chan'), axis=0, tiled=True)  16.6 us
  transfers between devices with their start and end apart: 3, of which 1 were waited for; matrix products, arithmetic and copies ran while one was open for 4% of the time, Pallas kernels for 0%

commit v1 on v0

v1 whole, which is shorter than its diff:
```python
import functools

import jax
import jax.numpy as jnp
import numpy as np
from jax import lax
from jax.experimental import pallas as pl
from jax.experimental.pallas import tpu as pltpu
from jax.sharding import PartitionSpec as P

SEG = 1024
SEGS = 4
REFS = 64
LAGS = 512
NN = 8
XN = 2
HALO = 16
CH = 128
NZ, NA, NB = 8, 4, 4
ROWS = SEGS * SEG // 128
GROUP = 16
MESH = pl.DeviceIdType.MESH
BF = jnp.bfloat16
F32 = jnp.float32


def forward_table():
    phase = (np.arange(SEG)[:, None] * np.arange(SEG // 2)[None, :]) % SEG
    theta = phase * (2.0 * np.pi / SEG)
    keep = (np.arange(SEG // 2) > 0)[None, :]
    return np.concatenate([np.cos(theta) * keep, -np.sin(theta)], 1).astype(BF)


def lag_table():
    phase = (np.arange(SEG // 2)[:, None] * (np.arange(LAGS) - LAGS // 2)[None, :]) % SEG
    theta = phase * (2.0 * np.pi / SEG)
    scale = 1.0 / np.sqrt(SEG // 2)
    table = np.concatenate([np.cos(theta) * scale, -np.sin(theta) * scale], 0).astype(BF)
    return (table.astype(np.float32) / SEGS).astype(BF)


def spectra_kernel(starts, ref_ids, export_loc, raw, table, white, export, picked, padded, seg, wide):
    base = (lax.axis_index("fibre") * (NZ * NA * NB) + lax.axis_index("chan")) * CH
    padded[:, : SEGS * SEG] = raw[...].astype(F32)
    padded[:, SEGS * SEG :] = jnp.zeros((CH, 128), F32)
    for s in range(SEGS):
        start = starts[s]
        first = pl.multiple_of((start // 128) * 128, 128)
        window = padded[:, pl.ds(first, SEG + 128)]
        turn = (SEG + 128) - (start - first)
        turned = pltpu.roll(window, turn, 1)
        seg[s * CH : (s + 1) * CH, :] = turned[:, :SEG].astype(BF)
    for s in range(SEGS):
        spectrum = jnp.dot(
            seg[s * CH : (s + 1) * CH, :], table[...], preferred_element_type=F32
        )
        power = jnp.sum(spectrum * spectrum, -1, keepdims=True) / (SEG // 2)
        spectrum = spectrum / jnp.sqrt(power + 1e-06)
        for j in range(SEG // 128):
            wide[pl.ds(s * 8 + j, CH, stride=ROWS), :] = spectrum[:, j * 128 : (j + 1) * 128]
    white[...] = wide[...].reshape(CH, ROWS, 128).astype(BF)
    export[0] = white[export_loc[0]]
    for r in range(REFS):
        local = ref_ids[r] - base
        mine = ((local >= 0) & (local < CH)).astype(F32)
        row = white[jnp.clip(local, 0, CH - 1)]
        picked[r] = (row.astype(F32) * mine).astype(BF)


def spectra(starts, ref_ids, export_loc, raw):
    smem = pl.BlockSpec(memory_space=pltpu.SMEM)
    vmem = pl.BlockSpec(memory_space=pltpu.VMEM)
    return pl.pallas_call(
        spectra_kernel,
        name="spectra",
        in_specs=[smem, smem, smem, vmem, vmem],
        out_specs=[vmem, vmem, vmem],
        out_shape=[
            jax.ShapeDtypeStruct((CH, ROWS, 128), BF),
            jax.ShapeDtypeStruct((1, ROWS, 128), BF),
            jax.ShapeDtypeStruct((REFS, ROWS, 128), BF),
        ],
        scratch_shapes=[
            pltpu.VMEM((CH, SEGS * SEG + 128), F32),
            pltpu.VMEM((CH * SEGS, SEG), BF),
            pltpu.VMEM((CH * ROWS, 128), F32),
        ],
        compiler_params=pltpu.CompilerParams(vmem_limit_bytes=40 << 20),
    )(starts, ref_ids, export_loc, raw, jnp.asarray(forward_table()))


def exchange_kernel(
    white, export, picked, halo, pool, refs,
    core_in, half, a_in, a_sum, b_in, b_sum, z_in, send, recv, core_send, core_recv,
):
    k = lax.axis_index("fibre")
    chan = lax.axis_index("chan")
    z, x, y = chan // (NA * NB), (chan // NB) % NA, chan % NB
    a = x * (1 - k) + y * k
    b = y * (1 - k) + x * k

    def at(zz, aa, bb):
        return zz * (NA * NB) + (aa * NB + bb) * (1 - k) + (bb * NB + aa) * k

    z_peer = [at((z + j) % NZ, a, b) for j in range(1, NZ)]
    a_peer = [at(z, (a + j) % NA, b) for j in range(1, NA)]
    b_peer = [at(z, a, (b + j) % NB) for j in range(1, NB)]
    up = (chan + 1) % (NZ * NA * NB)
    down = (chan + (NZ * NA * NB) - 1) % (NZ * NA * NB)
    own = z * (NA * NB) + a * NB + b

    barrier = pltpu.get_barrier_semaphore()
    peers = [(k, c) for c in z_peer + a_peer + b_peer + [up, down]] + [(1 - k, chan)]
    for peer in peers:
        pl.semaphore_signal(barrier, inc=1, device_id=peer, device_id_type=MESH)
    pl.semaphore_wait(barrier, len(peers))

    slot = [0]

    def start(src, dst, peer):
        i = slot[0]
        slot[0] += 1
        copy = pltpu.make_async_remote_copy(
            src_ref=src, dst_ref=dst, send_sem=send.at[i], recv_sem=recv.at[i],
            device_id=peer, device_id_type=MESH,
        )
        copy.start()
        return copy

    sent = []

    def arrive(copies):
        for copy in copies:
            copy.wait_recv()
        sent.extend(copies)

    partner = (1 - k, chan)
    whole = pool.reshape(2, NZ, NA, NB, ROWS, 128)

    core = start(picked.at[pl.ds((1 - k) * (REFS // 2), REFS // 2)], core_in, partner)
    mine = pltpu.make_async_copy(export, pool.at[pl.ds(k * CH + own, 1)], core_send)
    mine.start()
    pool_z = [start(export, pool.at[pl.ds(k * CH + own, 1)], (k, c)) for c in z_peer]
    halos = [
        start(white.at[pl.ds(CH - HALO, HALO)], halo.at[0], (k, up)),
        start(white.at[pl.ds(0, HALO)], halo.at[1], (k, down)),
    ]

    arrive([core])
    half[...] = picked[pl.ds(k * (REFS // 2), REFS // 2)] + core_in[...]
    a_rs = [
        start(half.at[pl.ds(((a + j) % NA) * 8, 8)], a_in.at[j - 1], (k, a_peer[j - 1]))
        for j in range(1, NA)
    ]

    mine.wait()
    arrive(pool_z)
    column = whole.at[k, :, a, b]
    pool_a = [start(column, column, (k, c)) for c in a_peer]
    pool_c = [start(column, column, partner)]

    arrive(a_rs)
    a_sum[...] = half[pl.ds(a * 8, 8)] + a_in[0] + a_in[1] + a_in[2]
    b_rs = [
        start(a_sum.at[pl.ds(((b + j) % NB) * 2, 2)], b_in.at[j - 1], (k, b_peer[j - 1]))
        for j in range(1, NB)
    ]

    arrive(pool_a)
    plane = whole.at[k, :, :, b]
    pool_b = [start(plane, plane, (k, b_peer[0])), start(plane, plane, (k, b_peer[2]))]
    for j in range(1, NA):
        got = whole.at[k, :, (a + NA - j) % NA, b]
        pool_c.append(start(got, got, partner))

    arrive(b_rs)
    b_sum[...] = a_sum[pl.ds(b * 2, 2)] + b_in[0] + b_in[1] + b_in[2]
    z_rs = [start(b_sum, z_in.at[j - 1], (k, z_peer[j - 1])) for j in range(1, NZ)]

    arrive(z_rs)
    total = b_sum[...]
    for j in range(NZ - 1):
        total = total + z_in[j]
    lead = k * (REFS // 2) + a * 8
    pair = refs.at[pl.ds(lead + b * 2, 2)]
    refs[pl.ds(lead + b * 2, 2)] = total
    refs_b = [start(pair, pair, (k, c)) for c in b_peer]

    arrive(pool_b)
    low = whole.at[k, pl.ds(0, NZ // 2), :, (b + NB - 1) % NB]
    high = whole.at[k, pl.ds(NZ // 2, NZ // 2), :, (b + 1) % NB]
    pool_r = [start(low, low, (k, b_peer[0])), start(high, high, (k, b_peer[2]))]
    for c in ((b + NB - 1) % NB, (b + 1) % NB):
        got = whole.at[k, :, :, c]
        pool_c.append(start(got, got, partner))

    arrive(refs_b)
    eight = refs.at[pl.ds(lead, 8)]
    refs_a = [start(eight, eight, (k, c)) for c in a_peer]
    refs_c = [start(eight, eight, partner)]

    arrive(refs_a)
    for j in range(1, NA):
        got = refs.at[pl.ds(k * (REFS // 2) + ((a + NA - j) % NA) * 8, 8)]
        refs_c.append(start(got, got, partner))
    arrive(pool_r)
    got = whole.at[k, :, :, (b + 2) % NB]
    pool_c.append(start(got, got, partner))

    arrive(halos)
    arrive(pool_c)
    arrive(refs_c)
    for copy in sent:
        copy.wait_send()


def exchange(white, export, picked):
    vmem = pl.BlockSpec(memory_space=pltpu.VMEM)
    copies = 1 + 7 + 2 + 3 + 3 + 1 + 3 + 2 + 3 + 7 + 3 + 2 + 2 + 3 + 1 + 3 + 1
    return pl.pallas_call(
        exchange_kernel,
        name="exchange",
        in_specs=[vmem] * 3,
        out_specs=[vmem] * 3,
        out_shape=[
            jax.ShapeDtypeStruct((2, HALO, ROWS, 128), BF),
            jax.ShapeDtypeStruct((2 * CH, ROWS, 128), BF),
            jax.ShapeDtypeStruct((REFS, ROWS, 128), BF),
        ],
        scratch_shapes=[
            pltpu.VMEM((REFS // 2, ROWS, 128), BF),
            pltpu.VMEM((REFS // 2, ROWS, 128), BF),
            pltpu.VMEM((NA - 1, 8, ROWS, 128), BF),
            pltpu.VMEM((8, ROWS, 128), BF),
            pltpu.VMEM((NB - 1, 2, ROWS, 128), BF),
            pltpu.VMEM((2, ROWS, 128), BF),
            pltpu.VMEM((NZ - 1, 2, ROWS, 128), BF),
            pltpu.SemaphoreType.DMA((copies,)),
            pltpu.SemaphoreType.DMA((copies,)),
            pltpu.SemaphoreType.DMA,
            pltpu.SemaphoreType.DMA,
        ],
        compiler_params=pltpu.CompilerParams(
            collective_id=0, has_side_effects=True, vmem_limit_bytes=40 << 20
        ),
    )(white, export, picked)


def correlate_kernel(
    near, cross, mask, white, halo, pool_hbm, refs_hbm, table, out,
    ext, pool, refs, wide, right, left, x, sem,
):
    step = pl.program_id(0)
    base = (lax.axis_index("fibre") * (NZ * NA * NB) + lax.axis_index("chan")) * CH

    @pl.when(step == 0)
    def _():
        copies = [
            pltpu.make_async_copy(refs_hbm, refs, sem.at[0]),
            pltpu.make_async_copy(white, ext.at[pl.ds(HALO, CH)], sem.at[1]),
            pltpu.make_async_copy(halo.at[0], ext.at[pl.ds(0, HALO)], sem.at[2]),
            pltpu.make_async_copy(halo.at[1], ext.at[pl.ds(HALO + CH, HALO)], sem.at[3]),
            pltpu.make_async_copy(pool_hbm, pool, sem.at[4]),
        ]
        for copy in copies:
            copy.start()
        copies[0].wait()
        wide[...] = refs[...].astype(F32).reshape(REFS * ROWS, 128)
        for row in range(ROWS):
            right[row] = wide[pl.ds(row, REFS, stride=ROWS), :].astype(BF)
        for copy in copies[1:]:
            copy.wait()

    for c in range(GROUP):
        chan = step * GROUP + c
        total = ext[HALO + chan].astype(F32)
        for n in range(NN):
            total = total + ext[near[chan, n] - base + HALO].astype(F32)
        count = 1.0 + NN
        for j in range(XN):
            p = cross[chan, j]
            swapped = (p & ~15) | ((p & 3) << 2) | ((p >> 2) & 3)
            live = mask[chan, j].astype(F32)
            total = total + pool[jnp.where(p < CH, p, swapped)].astype(F32) * live
            count = count + live
        left[c] = (total / count).astype(BF).astype(F32)

    for c in range(GROUP):
        for t in range(4):
            lhs = [
                jnp.broadcast_to(left[c, row : row + 1, :], (16, 128)).astype(BF)
                for row in range(t, ROWS, 4)
            ]
            for r in range(0, REFS, 16):
                rhs = [right[row, r : r + 16, :] for row in range(t, ROWS, 4)]
                p = [u * v for u, v in zip(lhs, rhs)]
                q = [
                    lhs[2 * s + 1] * rhs[2 * s] - lhs[2 * s] * rhs[2 * s + 1]
                    for s in range(SEGS)
                ]
                g = ((p[0] + p[1]) + (p[2] + p[3])) + ((p[4] + p[5]) + (p[6] + p[7]))
                h = (q[0] + q[1]) + (q[2] + q[3])
                lo = c * REFS + r
                x[lo : lo + 16, t * 128 : t * 128 + 128] = g
                x[lo : lo + 16, 512 + t * 128 : 512 + t * 128 + 128] = h
    y = jnp.dot(x[...], table[...], preferred_element_type=F32)
    out[...] = y.astype(BF).reshape(GROUP, REFS, LAGS)


def correlate(near_ids, cross_ids, cross_mask, white, halo, pool, refs):
    smem = pl.BlockSpec(memory_space=pltpu.SMEM)
    hbm = pl.BlockSpec(memory_space=pl.ANY)
    return pl.pallas_call(
        correlate_kernel,
        name="correlate",
        grid=(CH // GROUP,),
        in_specs=[smem, smem, smem, hbm, hbm, hbm, hbm, pl.BlockSpec((SEG, LAGS), lambda i: (0, 0))],
        out_specs=pl.BlockSpec((GROUP, REFS, LAGS), lambda i: (i, 0, 0)),
        out_shape=jax.ShapeDtypeStruct((CH, REFS, LAGS), BF),
        scratch_shapes=[
            pltpu.VMEM((CH + 2 * HALO, ROWS, 128), BF),
            pltpu.VMEM((2 * CH, ROWS, 128), BF),
            pltpu.VMEM((REFS, ROWS, 128), BF),
            pltpu.VMEM((REFS * ROWS, 128), F32),
            pltpu.VMEM((ROWS, REFS, 128), BF),
            pltpu.VMEM((GROUP, ROWS, 128), F32),
            pltpu.VMEM((GROUP * REFS, SEG), BF),
            pltpu.SemaphoreType.DMA((5,)),
        ],
        compiler_params=pltpu.CompilerParams(vmem_limit_bytes=40 << 20),
    )(near_ids, cross_ids, cross_mask, white, halo, pool, refs, jnp.asarray(lag_table()))


def per_device(raw, starts, ref_ids, near_ids, cross_ids, cross_mask, export_loc):
    white, export, picked = spectra(starts, ref_ids, export_loc, raw)
    halo, pool, refs = exchange(white, export, picked)
    return correlate(near_ids, cross_ids, cross_mask, white, halo, pool, refs)


def solution(mesh):
    split = ("fibre", "chan")
    in_specs = (P(split, None), P(), P(), P(split, None), P(split, None), P(split, None), P(split))
    return jax.shard_map(
        per_device, mesh=mesh, in_specs=in_specs, out_specs=P(split, None, None), check_vma=False
    )
```

time: 316 us -> 78.4 us (0.25)
  blocking collectives: 88.9 us -> 0 us
  matrix products: 80.2 us -> 0 us
  local copies, waits for them, and re-layouts: 79.5 us -> 6.48 us
  Pallas kernels: 0 us -> 71 us
  other arithmetic: 22.8 us -> 0 us
  between operations: 21.9 us -> 0.69 us
  waiting for transfers between devices: 16.6 us -> 0 us
  starting transfers between devices: 5.32 us -> 0 us
    psum x1 -> x0, blocking collectives: 88.9 us -> none  [per_device(): references = lax.psum(selected, ('fibre', 'chan')).astype(jnp.bfloat16)]
    dot_general x24 -> x0, matrix products: 80.2 us -> none  [the longest x4 23.2 us: correlate(): jnp.dot(cross.reshape(group * REFS, SEG), kernel, preferred_element_type=...]
    pallas_call x0 -> x3, Pallas kernels: none -> 71 us  [the longest x1 38.9 us: exchange(): pl.pallas_call(exchange_kernel, name='exchange', in_specs=[vmem] * 3, out...]
    add x4 -> x0, local copies, waits for them, and re-layouts: 27.7 us -> none  [correlate(): jnp.einsum('csf,rsf->crf', a_re, ref_re, preferred_element_type=jnp.float32)]
    sub x4 -> x0, local copies, waits for them, and re-layouts: 27.7 us -> none  [correlate(): jnp.einsum('csf,rsf->crf', a_im, ref_re, preferred_element_type=jnp.float32)]
    another operation x4 -> x0, other arithmetic: 20.5 us -> none
    all_gather x1 -> x0, waiting for transfers between devices: 16.6 us -> none  [per_device(): piece = lax.all_gather(exported, ('fibre', 'chan'), axis=0, tiled=True)]
    dynamic_update_slice x4 -> x0, local copies, waits for them, and re-layouts: 6.22 us -> none  [per_device(): lax.map(correlate, smoothed.reshape(local_ch // group, group, SEGS, SEG))]
  transfers between devices with their start and end apart: 3 -> 0, of which waited for: 1 -> 0; matrix products, arithmetic and copies ran while one was open for 4% -> 0% of each run, Pallas kernels for 0% -> 0%
where the time goes in v1:
time: 78.4 us; the launch traced here: 78.1 us
  Pallas kernels  71 us (91%)
  local copies, waits for them, and re-layouts  6.48 us (8%)
    pallas_call x1, Pallas kernels, exchange(): pl.pallas_call(exchange_kernel, name='exchange', in_specs=[vmem] * 3, out...  38.9 us
    pallas_call x1, Pallas kernels, correlate(): pl.pallas_call(correlate_kernel, name='correlate', grid=(CH // GROUP,), i...  27.8 us
    unnamed x13, local copies, waits for them, and re-layouts  6.48 us
    pallas_call x1, Pallas kernels, spectra(): pl.pallas_call(spectra_kernel, name='spectra', in_specs=[smem, smem, smem...  4.2 us

profile of v1, /device:TPU:1, one launch (start us, length us, event | category | flops | bytes accessed | tf_op | source)
XLA Modules:
  0.0 78.1 jit_solution(11997578427989367687)
XLA Ops:
  0.7 0.8 %copy.10.near = s32[128,8]{1,0:T(8,128)S(1)} copy(s32[128,8]{0,1:T(8,128)} %param.12) | data formatting | bytes 8192 | tf_op args[3]
  1.4 0.8 %copy.11.cross = s32[128,2]{1,0:T(8,128)S(1)} copy(s32[128,2]{0,1:T(2,128)} %param.13) | data formatting | bytes 2048 | tf_op args[4]
  2.2 0.8 %copy.12.mask = s32[128,2]{1,0:T(8,128)S(1)} copy(s32[128,2]{0,1:T(2,128)} %param.14) | data formatting | bytes 2048 | tf_op args[5]
  3.0 0.0 copy-start
  3.0 1.6 %copy-done = bf16[1024,1024]{1,0:T(8,128)(2,1)S(1)} copy-done((bf16[1024,1024]{1,0:T(8,128)(2,1)S(1)}, bf16[1024,1024]{1,0:T(8,128)(2,1)}, u32[]{:S(2)}) %copy-start) | copy-done | bytes 2097176
  4.6 0.0 copy-start.2
  4.6 1.2 %copy-done.2 = bf16[128,4096]{1,0:T(8,128)(2,1)S(1)} copy-done((bf16[128,4096]{1,0:T(8,128)(2,1)S(1)}, bf16[128,4096]{1,0:T(8,128)(2,1)}, u32[]{:S(2)}) %copy-start.2) | copy-done | bytes 1048600
  5.8 0.0 copy-start.3
  5.8 0.7 copy-done.3
  6.5 0.0 copy-start.4
  6.5 0.7 copy-done.4
  7.1 0.0 copy-start.1
  7.1 4.2 %spectra.1 = (bf16[128,32,128]{2,1,0:T(8,128)(2,1)S(1)}, bf16[1,32,128]{2,1,0:T(8,128)(2,1)S(1)}, bf16[64,32,128]{2,1,0:T(8,128)(2,1)S(1)}) custom-call(s32[4]{0:T(128)S(1)} %copy-done.3, s32[64]{0:T(128)S(1)} %copy-done.4, s32[1]{0:T(128)S(6)} %copy.13.export_loc, bf16[128,4096]{1,0:T(8,128)(2,1)S(1)} %copy-done.2, bf16[1024,1024]{1,0:T(8,128)(2,1)S(1)} %copy-done), custom_call_target="tpu_custom_call" | custom-call | tf_op jit(solution)/shard_map/spectra/pallas_call | solution.py:73
  11.3 38.9 %exchange.1 = (bf16[2,16,32,128]{3,2,1,0:T(8,128)(2,1)S(1)}, bf16[256,32,128]{2,1,0:T(8,128)(2,1)S(1)}, bf16[64,32,128]{2,1,0:T(8,128)(2,1)S(1)}) custom-call(bf16[128,32,128]{2,1,0:T(8,128)(2,1)S(1)} %get-tuple-element.11.white, bf16[1,32,128]{2,1,0:T(8,128)(2,1)S(1)} %get-tuple-element.12.export, bf16[64,32,128]{2,1,0:T(8,128)(2,1)S(1)} %get-tuple-element.13.picked), custom_call_target="tpu_custom_call" | custom-call | tf_op jit(solution)/shard_map/exchange/pallas_call | solution.py:220
  50.3 0.0 copy-done.1
  50.3 27.8 %correlate.1 = bf16[128,64,512]{2,1,0:T(8,128)(2,1)} custom-call(s32[128,8]{1,0:T(8,128)S(1)} %copy.10.near, s32[128,2]{1,0:T(8,128)S(1)} %copy.11.cross, s32[128,2]{1,0:T(8,128)S(1)} %copy.12.mask, bf16[128,32,128]{2,1,0:T(8,128)(2,1)S(1)} %get-tuple-element.11.white, bf16[2,16,32,128]{3,2,1,0:T(8,128)(2,1)S(1)} %get-tuple-element.14.halo, ...), custom_call_target="tpu_custom_call" | custom-call | tf_op jit(solution)/shard_map/correlate/pallas_call | solution.py:313
Async XLA Ops:
  3.0 1.6 %copy-start = (bf16[1024,1024]{1,0:T(8,128)(2,1)S(1)}, bf16[1024,1024]{1,0:T(8,128)(2,1)}, u32[]{:S(2)}) copy-start(bf16[1024,1024]{1,0:T(8,128)(2,1)} %constant.4.clone.table) | copy-start | bytes 6291460
  4.6 1.2 %copy-start.2 = (bf16[128,4096]{1,0:T(8,128)(2,1)S(1)}, bf16[128,4096]{1,0:T(8,128)(2,1)}, u32[]{:S(2)}) copy-start(bf16[128,4096]{1,0:T(8,128)(2,1)} %raw.1) | copy-start | bytes 3145732
  5.8 0.7 copy-start.3
  6.5 0.7 copy-start.4
  7.1 43.1 %copy-start.1 = (bf16[1024,512]{1,0:T(8,128)(2,1)S(1)}, bf16[1024,512]{1,0:T(8,128)(2,1)}, u32[]{:S(2)}) copy-start(bf16[1024,512]{1,0:T(8,128)(2,1)} %constant.5.clone.table) | copy-start | bytes 3145732

commit v2 on v1

v2 whole, which is shorter than its diff:
```python
import functools

import jax
import jax.numpy as jnp
import numpy as np
from jax import lax
from jax.experimental import pallas as pl
from jax.experimental.pallas import tpu as pltpu
from jax.sharding import PartitionSpec as P

SEG = 1024
SEGS = 4
REFS = 64
LAGS = 512
NN = 8
XN = 2
HALO = 16
CH = 128
NZ, NA, NB = 8, 4, 4
ROWS = SEGS * SEG // 128
GROUP = 16
MESH = pl.DeviceIdType.MESH
BF = jnp.bfloat16
F32 = jnp.float32


def forward_table():
    phase = (np.arange(SEG)[:, None] * np.arange(SEG // 2)[None, :]) % SEG
    theta = phase * (2.0 * np.pi / SEG)
    keep = (np.arange(SEG // 2) > 0)[None, :]
    return np.concatenate([np.cos(theta) * keep, -np.sin(theta)], 1).astype(BF)


def lag_table():
    phase = (np.arange(SEG // 2)[:, None] * (np.arange(LAGS) - LAGS // 2)[None, :]) % SEG
    theta = phase * (2.0 * np.pi / SEG)
    scale = 1.0 / np.sqrt(SEG // 2)
    table = np.concatenate([np.cos(theta) * scale, -np.sin(theta) * scale], 0).astype(BF)
    return (table.astype(np.float32) / SEGS).astype(BF)


def spectra_kernel(ints_in, raw, table_in, white, export, picked, ints, samples, table, seg, wide, load):
    base = (lax.axis_index("fibre") * (NZ * NA * NB) + lax.axis_index("chan")) * CH
    loads = [
        pltpu.make_async_copy(raw, samples.at[:, pl.ds(0, SEGS * SEG)], load.at[0]),
        pltpu.make_async_copy(ints_in, ints, load.at[1]),
        pltpu.make_async_copy(table_in, table, load.at[2]),
    ]
    for copy in loads:
        copy.start()
    samples[:, SEGS * SEG :] = jnp.zeros((CH, 128), BF)
    loads[0].wait()
    loads[1].wait()
    for s in range(SEGS):
        begin = ints[REFS + s]
        lead = pl.multiple_of((begin // 128) * 128, 128)
        window = samples[:, pl.ds(lead, SEG + 128)].astype(F32)
        cut = pltpu.roll(window, (SEG + 128) - (begin - lead), 1)[:, :SEG]
        seg[s * CH : (s + 1) * CH, :] = cut.astype(BF)
    loads[2].wait()
    for s in range(SEGS):
        spectrum = jnp.dot(
            seg[s * CH : (s + 1) * CH, :], table[...], preferred_element_type=F32
        )
        power = jnp.sum(spectrum * spectrum, -1, keepdims=True) / (SEG // 2)
        spectrum = spectrum / jnp.sqrt(power + 1e-06)
        for j in range(SEG // 128):
            wide[pl.ds(s * 8 + j, CH, stride=ROWS), :] = spectrum[:, j * 128 : (j + 1) * 128]

    def rows(channel):
        first = pl.multiple_of(channel * ROWS, ROWS)
        return wide[pl.ds(first, ROWS), :]

    def pick(r, carry):
        local = ints[r] - base
        mine = ((local >= 0) & (local < CH)).astype(F32)
        picked[r] = (rows(jnp.clip(local, 0, CH - 1)) * mine).astype(BF)
        return carry

    lax.fori_loop(0, REFS, pick, 0, unroll=8)
    export[0] = rows(ints[REFS + SEGS]).astype(BF)
    white[...] = wide[...].reshape(CH, ROWS, 128).astype(BF)


def spectra(ref_ids, starts, export_loc, raw):
    vmem = pl.BlockSpec(memory_space=pltpu.VMEM)
    hbm = pl.BlockSpec(memory_space=pl.ANY)
    fill = jnp.zeros((128 - REFS - SEGS - 1,), jnp.int32)
    ints = jnp.concatenate([ref_ids, starts, export_loc, fill])
    return pl.pallas_call(
        spectra_kernel,
        name="spectra",
        in_specs=[hbm] * 3,
        out_specs=[vmem] * 3,
        out_shape=[
            jax.ShapeDtypeStruct((CH, ROWS, 128), BF),
            jax.ShapeDtypeStruct((1, ROWS, 128), BF),
            jax.ShapeDtypeStruct((REFS, ROWS, 128), BF),
        ],
        scratch_shapes=[
            pltpu.SMEM((128,), jnp.int32),
            pltpu.VMEM((CH, SEGS * SEG + 128), BF),
            pltpu.VMEM((SEG, SEG), BF),
            pltpu.VMEM((CH * SEGS, SEG), BF),
            pltpu.VMEM((CH * ROWS, 128), F32),
            pltpu.SemaphoreType.DMA((3,)),
        ],
        compiler_params=pltpu.CompilerParams(vmem_limit_bytes=16 << 20),
    )(
        ints,
        pltpu.with_memory_space_constraint(raw, pltpu.HBM),
        pltpu.with_memory_space_constraint(jnp.asarray(forward_table()), pltpu.HBM),
    )


def exchange_kernel(
    white, export, picked, ext, pool, refs,
    core_in, half, a_in, a_sum, b_in, b_sum, z_in, send, recv,
):
    k = lax.axis_index("fibre")
    chan = lax.axis_index("chan")
    z, x, y = chan // (NA * NB), (chan // NB) % NA, chan % NB
    a = x * (1 - k) + y * k
    b = y * (1 - k) + x * k

    def at(zz, aa, bb):
        return zz * (NA * NB) + (aa * NB + bb) * (1 - k) + (bb * NB + aa) * k

    z_peer = [at((z + j) % NZ, a, b) for j in range(1, NZ)]
    a_peer = [at(z, (a + j) % NA, b) for j in range(1, NA)]
    b_peer = [at(z, a, (b + j) % NB) for j in range(1, NB)]
    up = (chan + 1) % (NZ * NA * NB)
    down = (chan + (NZ * NA * NB) - 1) % (NZ * NA * NB)
    own = z * (NA * NB) + a * NB + b

    barrier = pltpu.get_barrier_semaphore()
    peers = [(k, c) for c in z_peer + a_peer + b_peer + [up, down]] + [(1 - k, chan)]
    for peer in peers:
        pl.semaphore_signal(barrier, inc=1, device_id=peer, device_id_type=MESH)

    slot = [0]

    def start(src, dst, peer):
        i = slot[0]
        slot[0] += 1
        copy = pltpu.make_async_remote_copy(
            src_ref=src, dst_ref=dst, send_sem=send.at[i], recv_sem=recv.at[i],
            device_id=peer, device_id_type=MESH,
        )
        copy.start()
        return copy

    sent = []

    def arrive(copies):
        for copy in copies:
            copy.wait_recv()
        sent.extend(copies)

    partner = (1 - k, chan)
    whole = pool.reshape(2, NZ, NA, NB, ROWS, 128)

    pool[pl.ds(k * CH + own, 1)] = export[...]
    pl.semaphore_wait(barrier, len(peers))
    core = start(picked.at[pl.ds((1 - k) * (REFS // 2), REFS // 2)], core_in, partner)
    mine = pool.at[pl.ds(k * CH + own, 1)]
    pool_z = [start(export, mine, (k, c)) for c in z_peer]
    halos = [
        start(white.at[pl.ds(CH - HALO, HALO)], ext.at[pl.ds(0, HALO)], (k, up)),
        start(white.at[pl.ds(0, HALO)], ext.at[pl.ds(HALO + CH, HALO)], (k, down)),
    ]

    arrive([core])
    half[...] = picked[pl.ds(k * (REFS // 2), REFS // 2)] + core_in[...]
    a_rs = [
        start(half.at[pl.ds(((a + j) % NA) * 8, 8)], a_in.at[j - 1], (k, a_peer[j - 1]))
        for j in range(1, NA)
    ]

    arrive(pool_z)
    column = whole.at[k, :, a, b]
    pool_a = [start(column, column, (k, c)) for c in a_peer]
    pool_c = [start(column, column, partner)]
    ext[HALO : HALO + CH] = white[...]

    arrive(a_rs)
    a_sum[...] = half[pl.ds(a * 8, 8)] + a_in[0] + a_in[1] + a_in[2]
    b_rs = [
        start(a_sum.at[pl.ds(((b + j) % NB) * 2, 2)], b_in.at[j - 1], (k, b_peer[j - 1]))
        for j in range(1, NB)
    ]

    arrive(b_rs)
    b_sum[...] = a_sum[pl.ds(b * 2, 2)] + b_in[0] + b_in[1] + b_in[2]
    z_rs = [start(b_sum, z_in.at[j - 1], (k, z_peer[j - 1])) for j in range(1, NZ)]

    arrive(pool_a)
    plane = whole.at[k, :, :, b]
    pool_b = [start(plane, plane, (k, b_peer[0])), start(plane, plane, (k, b_peer[2]))]
    for j in range(1, NA):
        got = whole.at[k, :, (a + NA - j) % NA, b]
        pool_c.append(start(got, got, partner))

    arrive(z_rs)
    total = b_sum[...]
    for j in range(NZ - 1):
        total = total + z_in[j]
    lead = k * (REFS // 2) + a * 8
    pair = refs.at[pl.ds(lead + b * 2, 2)]
    refs[pl.ds(lead + b * 2, 2)] = total
    refs_b = [start(pair, pair, (k, c)) for c in b_peer]

    arrive(pool_b)
    low = whole.at[k, pl.ds(0, NZ // 2), :, (b + NB - 1) % NB]
    high = whole.at[k, pl.ds(NZ // 2, NZ // 2), :, (b + 1) % NB]
    pool_r = [start(low, low, (k, b_peer[0])), start(high, high, (k, b_peer[2]))]

    arrive(refs_b)
    eight = refs.at[pl.ds(lead, 8)]
    refs_a = [start(eight, eight, (k, c)) for c in a_peer]
    refs_c = [start(eight, eight, partner)]
    for c in ((b + NB - 1) % NB, (b + 1) % NB):
        got = whole.at[k, :, :, c]
        pool_c.append(start(got, got, partner))

    arrive(pool_r)
    got = whole.at[k, :, :, (b + 2) % NB]
    pool_c.append(start(got, got, partner))

    for j in range(1, NA):
        arrive([refs_a[j - 1]])
        got = refs.at[pl.ds(k * (REFS // 2) + ((a + NA - j) % NA) * 8, 8)]
        refs_c.append(start(got, got, partner))

    arrive(halos)
    arrive(pool_c)
    arrive(refs_c)
    for copy in sent:
        copy.wait_send()


def exchange(white, export, picked):
    vmem = pl.BlockSpec(memory_space=pltpu.VMEM)
    copies = 1 + 3 + 7 + 3 + 2 + 7 + 3 + 1 + 3 + 2 + 3 + 3 + 1 + 2 + 2 + 3 + 1
    return pl.pallas_call(
        exchange_kernel,
        name="exchange",
        in_specs=[vmem] * 3,
        out_specs=[vmem] * 3,
        out_shape=[
            jax.ShapeDtypeStruct((CH + 2 * HALO, ROWS, 128), BF),
            jax.ShapeDtypeStruct((2 * CH, ROWS, 128), BF),
            jax.ShapeDtypeStruct((REFS, ROWS, 128), BF),
        ],
        scratch_shapes=[
            pltpu.VMEM((REFS // 2, ROWS, 128), BF),
            pltpu.VMEM((REFS // 2, ROWS, 128), BF),
            pltpu.VMEM((NA - 1, 8, ROWS, 128), BF),
            pltpu.VMEM((8, ROWS, 128), BF),
            pltpu.VMEM((NB - 1, 2, ROWS, 128), BF),
            pltpu.VMEM((2, ROWS, 128), BF),
            pltpu.VMEM((NZ - 1, 2, ROWS, 128), BF),
            pltpu.SemaphoreType.DMA((copies,)),
            pltpu.SemaphoreType.DMA((copies,)),
        ],
        compiler_params=pltpu.CompilerParams(
            collective_id=0, has_side_effects=True, vmem_limit_bytes=24 << 20
        ),
    )(white, export, picked)


def correlate_kernel(
    near_in, cross_in, mask_in, ext, pool, refs, table, out,
    near, cross, mask, wide, right, left, x, rows, load, store,
):
    base = (lax.axis_index("fibre") * (NZ * NA * NB) + lax.axis_index("chan")) * CH
    loads = [
        pltpu.make_async_copy(near_in, near, load.at[0]),
        pltpu.make_async_copy(cross_in, cross, load.at[1]),
        pltpu.make_async_copy(mask_in, mask, load.at[2]),
    ]
    for copy in loads:
        copy.start()
    wide[...] = refs[...].astype(F32).reshape(REFS * ROWS, 128)
    for row in range(ROWS):
        right[row] = wide[pl.ds(row, REFS, stride=ROWS), :].astype(BF)
    for copy in loads:
        copy.wait()
    steps = CH // GROUP

    def put(step):
        return pltpu.make_async_copy(
            rows.at[step % 2], out.at[pl.ds(step * GROUP, GROUP)], store.at[step % 2]
        )

    def body(step, carry):
        for c in range(GROUP):
            chan = step * GROUP + c
            total = ext[HALO + chan].astype(F32)
            for n in range(NN):
                total = total + ext[near[n, chan] - base + HALO].astype(F32)
            count = 1.0 + NN
            for j in range(XN):
                p = cross[j, chan]
                swapped = (p & ~15) | ((p & 3) << 2) | ((p >> 2) & 3)
                live = mask[j, chan].astype(F32)
                total = total + pool[jnp.where(p < CH, p, swapped)].astype(F32) * live
                count = count + live
            left[c] = (total / count).astype(BF).astype(F32)

        for c in range(GROUP):
            for t in range(4):
                lhs = [
                    jnp.broadcast_to(left[c, row : row + 1, :], (16, 128)).astype(BF)
                    for row in range(t, ROWS, 4)
                ]
                for r in range(0, REFS, 16):
                    rhs = [right[row, r : r + 16, :] for row in range(t, ROWS, 4)]
                    p = [u * v for u, v in zip(lhs, rhs)]
                    q = [
                        lhs[2 * s + 1] * rhs[2 * s] - lhs[2 * s] * rhs[2 * s + 1]
                        for s in range(SEGS)
                    ]
                    g = ((p[0] + p[1]) + (p[2] + p[3])) + ((p[4] + p[5]) + (p[6] + p[7]))
                    h = (q[0] + q[1]) + (q[2] + q[3])
                    lo = c * REFS + r
                    x[lo : lo + 16, t * 128 : t * 128 + 128] = g
                    x[lo : lo + 16, 512 + t * 128 : 512 + t * 128 + 128] = h

        @pl.when(step >= 2)
        def _():
            put(step - 2).wait()

        y = jnp.dot(x[...], table[...], preferred_element_type=F32)
        rows[step % 2] = y.astype(BF).reshape(GROUP, REFS, LAGS)
        put(step).start()
        return carry

    lax.fori_loop(0, steps, body, 0)
    put(steps - 2).wait()
    put(steps - 1).wait()


def correlate(near_ids, cross_ids, cross_mask, ext, pool, refs):
    vmem = pl.BlockSpec(memory_space=pltpu.VMEM)
    hbm = pl.BlockSpec(memory_space=pl.ANY)
    return pl.pallas_call(
        correlate_kernel,
        name="correlate",
        in_specs=[hbm] * 3 + [vmem] * 4,
        out_specs=hbm,
        out_shape=jax.ShapeDtypeStruct((CH, REFS, LAGS), BF),
        scratch_shapes=[
            pltpu.SMEM((NN, CH), jnp.int32),
            pltpu.SMEM((XN, CH), jnp.int32),
            pltpu.SMEM((XN, CH), jnp.int32),
            pltpu.VMEM((REFS * ROWS, 128), F32),
            pltpu.VMEM((ROWS, REFS, 128), BF),
            pltpu.VMEM((GROUP, ROWS, 128), F32),
            pltpu.VMEM((GROUP * REFS, SEG), BF),
            pltpu.VMEM((2, GROUP, REFS, LAGS), BF),
            pltpu.SemaphoreType.DMA((3,)),
            pltpu.SemaphoreType.DMA((2,)),
        ],
        compiler_params=pltpu.CompilerParams(vmem_limit_bytes=24 << 20),
    )(near_ids.T, cross_ids.T, cross_mask.T, ext, pool, refs, jnp.asarray(lag_table()))


def per_device(raw, starts, ref_ids, near_ids, cross_ids, cross_mask, export_loc):
    white, export, picked = spectra(ref_ids, starts, export_loc, raw)
    ext, pool, refs = exchange(white, export, picked)
    return correlate(near_ids, cross_ids, cross_mask, ext, pool, refs)


def solution(mesh):
    split = ("fibre", "chan")
    in_specs = (P(split, None), P(), P(), P(split, None), P(split, None), P(split, None), P(split))
    return jax.shard_map(
        per_device, mesh=mesh, in_specs=in_specs, out_specs=P(split, None, None), check_vma=False
    )
```

time: 78.4 us -> 69.6 us (0.89)
  local copies, waits for them, and re-layouts: 6.48 us -> 0.02 us
  Pallas kernels: 71 us -> 68 us
    unnamed x13 -> x8, local copies, waits for them, and re-layouts: 6.48 us -> 0.02 us
    pallas_call x2, Pallas kernels: 32 us -> 29.6 us  [the longest x1 24.5 us: correlate(): pl.pallas_call(correlate_kernel, name='correlate', in_specs=[hbm] * 3 + [...]
where the time goes in v2:
time: 69.6 us; the launch traced here: 69.5 us
  Pallas kernels  68 us (98%)
  other arithmetic  0.75 us (1%)
  between operations  0.72 us (1%)
    pallas_call x1, Pallas kernels, exchange(): pl.pallas_call(exchange_kernel, name='exchange', in_specs=[vmem] * 3, out...  38.4 us
    pallas_call x1, Pallas kernels, correlate(): pl.pallas_call(correlate_kernel, name='correlate', in_specs=[hbm] * 3 + [...  24.5 us
    pallas_call x1, Pallas kernels, spectra(): pl.pallas_call(spectra_kernel, name='spectra', in_specs=[hbm] * 3, out_sp...  5.14 us

profile of v2, /device:TPU:1, one launch (start us, length us, event | category | flops | bytes accessed | tf_op | source)
XLA Modules:
  0.0 69.5 jit_solution(5848005826227212095)
XLA Ops:
  0.7 0.8 %pad_add_fusion.ints_in = s32[128]{0:T(128)S(1)} fusion(s32[59]{0:T(128)S(1)} %broadcast_in_dim.3, s32[1]{0:T(128)S(6)} %copy.10, s32[4]{0:T(128)} %param.10, s32[64]{0:T(128)} %param.11), kind=kLoop, calls=%fused_computation | loop fusion | flops 384 | bytes 1024 | tf_op jit(solution)/shard_map/concatenate | solution.py:89
  1.4 0.0 copy-start
  1.4 0.0 copy-start.1
  1.4 0.0 copy-start.2
  1.4 0.0 copy-start.3
  1.4 5.1 %spectra.1 = (bf16[128,32,128]{2,1,0:T(8,128)(2,1)S(1)}, bf16[1,32,128]{2,1,0:T(8,128)(2,1)S(1)}, bf16[64,32,128]{2,1,0:T(8,128)(2,1)S(1)}) custom-call(s32[128]{0:T(128)S(1)} %pad_add_fusion.ints_in, bf16[128,4096]{1,0:T(8,128)(2,1)} %raw.1, bf16[1024,1024]{1,0:T(8,128)(2,1)} %constant.6.clone.table_in), custom_call_target="tpu_custom_call" | custom-call | tf_op jit(solution)/shard_map/spectra/pallas_call | solution.py:90
  6.6 38.4 %exchange.1 = (bf16[160,32,128]{2,1,0:T(8,128)(2,1)S(1)}, bf16[256,32,128]{2,1,0:T(8,128)(2,1)S(1)}, bf16[64,32,128]{2,1,0:T(8,128)(2,1)S(1)}) custom-call(bf16[128,32,128]{2,1,0:T(8,128)(2,1)S(1)} %get-tuple-element.11.white, bf16[1,32,128]{2,1,0:T(8,128)(2,1)S(1)} %get-tuple-element.12.export, bf16[64,32,128]{2,1,0:T(8,128)(2,1)S(1)} %get-tuple-element.13.picked), custom_call_target="tpu_custom_call" | custom-call | tf_op jit(solution)/shard_map/exchange/pallas_call | solution.py:245
  45.0 0.0 copy-done
  45.0 0.0 copy-done.1
  45.0 0.0 copy-done.2
  45.0 0.0 copy-done.3
  45.0 24.5 %correlate.1 = bf16[128,64,512]{2,1,0:T(8,128)(2,1)} custom-call(s32[8,128]{1,0:T(8,128)S(1)} %bitcast.3, s32[2,128]{1,0:T(2,128)S(1)} %bitcast.4, s32[2,128]{1,0:T(2,128)S(1)} %bitcast.5, bf16[160,32,128]{2,1,0:T(8,128)(2,1)S(1)} %get-tuple-element.14.ext, bf16[256,32,128]{2,1,0:T(8,128)(2,1)S(1)} %get-tuple-element.15.pool, ...), custom_call_target="tpu_custom_call" | custom-call | tf_op jit(solution)/shard_map/correlate/pallas_call | solution.py:347
  (1 shorter events, 0.0 us)
Async XLA Ops:
  1.4 43.6 %copy-start = (bf16[1024,512]{1,0:T(8,128)(2,1)S(1)}, bf16[1024,512]{1,0:T(8,128)(2,1)}, u32[]{:S(2)}) copy-start(bf16[1024,512]{1,0:T(8,128)(2,1)} %constant.7.clone.table) | copy-start | bytes 3145732
  1.4 43.6 %copy-start.1 = (s32[128,8]{0,1:T(8,128)S(1)}, s32[128,8]{0,1:T(8,128)}, u32[]{:S(2)}) copy-start(s32[128,8]{0,1:T(8,128)} %param.12) | copy-start | bytes 12292
  1.4 43.6 %copy-start.2 = (s32[128,2]{0,1:T(2,128)S(1)}, s32[128,2]{0,1:T(2,128)}, u32[]{:S(2)}) copy-start(s32[128,2]{0,1:T(2,128)} %param.13) | copy-start | bytes 3076
  1.4 43.6 %copy-start.3 = (s32[128,2]{0,1:T(2,128)S(1)}, s32[128,2]{0,1:T(2,128)}, u32[]{:S(2)}) copy-start(s32[128,2]{0,1:T(2,128)} %param.14) | copy-start | bytes 3076

commit v3 on v2

--- a/solution.py
+++ b/solution.py
@@ -19,6 +19,7 @@
 NZ, NA, NB = 8, 4, 4
 ROWS = SEGS * SEG // 128
 GROUP = 16
+HALF = 8
 MESH = pl.DeviceIdType.MESH
 BF = jnp.bfloat16
 F32 = jnp.float32
@@ -269,9 +270,26 @@
     )(white, export, picked)
 
 
+def products(left, right, c):
+    low = [[None] * 4 for _ in range(REFS // 16)]
+    high = [[None] * 4 for _ in range(REFS // 16)]
+    for t in range(4):
+        lhs = [
+            jnp.broadcast_to(left[c, row : row + 1, :], (16, 128)).astype(BF)
+            for row in range(t, ROWS, 4)
+        ]
+        for r in range(REFS // 16):
+            rhs = [right[row, r * 16 : r * 16 + 16, :] for row in range(t, ROWS, 4)]
+            p = [u * v for u, v in zip(lhs, rhs)]
+            q = [lhs[2 * s + 1] * rhs[2 * s] - lhs[2 * s] * rhs[2 * s + 1] for s in range(SEGS)]
+            low[r][t] = ((p[0] + p[1]) + (p[2] + p[3])) + ((p[4] + p[5]) + (p[6] + p[7]))
+            high[r][t] = (q[0] + q[1]) + (q[2] + q[3])
+    return jnp.concatenate([jnp.concatenate(low[r] + high[r], 1) for r in range(REFS // 16)], 0)
+
+
 def correlate_kernel(
     near_in, cross_in, mask_in, ext, pool, refs, table, out,
-    near, cross, mask, wide, right, left, x, rows, load, store,
+    near, cross, mask, wide, right, left, rows, load, store,
 ):
     base = (lax.axis_index("fibre") * (NZ * NA * NB) + lax.axis_index("chan")) * CH
     loads = [
@@ -299,40 +317,27 @@
             total = ext[HALO + chan].astype(F32)
             for n in range(NN):
                 total = total + ext[near[n, chan] - base + HALO].astype(F32)
-            count = 1.0 + NN
+            links = 0
             for j in range(XN):
                 p = cross[j, chan]
                 swapped = (p & ~15) | ((p & 3) << 2) | ((p >> 2) & 3)
-                live = mask[j, chan].astype(F32)
-                total = total + pool[jnp.where(p < CH, p, swapped)].astype(F32) * live
-                count = count + live
-            left[c] = (total / count).astype(BF).astype(F32)
-
-        for c in range(GROUP):
-            for t in range(4):
-                lhs = [
-                    jnp.broadcast_to(left[c, row : row + 1, :], (16, 128)).astype(BF)
-                    for row in range(t, ROWS, 4)
-                ]
-                for r in range(0, REFS, 16):
-                    rhs = [right[row, r : r + 16, :] for row in range(t, ROWS, 4)]
-                    p = [u * v for u, v in zip(lhs, rhs)]
-                    q = [
-                        lhs[2 * s + 1] * rhs[2 * s] - lhs[2 * s] * rhs[2 * s + 1]
-                        for s in range(SEGS)
-                    ]
-                    g = ((p[0] + p[1]) + (p[2] + p[3])) + ((p[4] + p[5]) + (p[6] + p[7]))
-                    h = (q[0] + q[1]) + (q[2] + q[3])
-                    lo = c * REFS + r
-                    x[lo : lo + 16, t * 128 : t * 128 + 128] = g
-                    x[lo : lo + 16, 512 + t * 128 : 512 + t * 128 + 128] = h
+                live = mask[j, chan]
+                total = total + pool[jnp.where(p < CH, p, swapped)].astype(F32) * live.astype(F32)
+                links = links + live
+            share = jnp.where(links == 0, 1.0 / 9, jnp.where(links == 1, 0.1, 1.0 / 11)).astype(F32)
+            left[c] = (total * share).astype(BF).astype(F32)
 
         @pl.when(step >= 2)
         def _():
             put(step - 2).wait()
 
-        y = jnp.dot(x[...], table[...], preferred_element_type=F32)
-        rows[step % 2] = y.astype(BF).reshape(GROUP, REFS, LAGS)
+        cross_spectra = [
+            jnp.concatenate([products(left, right, c) for c in range(h, h + HALF)], 0)
+            for h in range(0, GROUP, HALF)
+        ]
+        for h, spectrum in enumerate(cross_spectra):
+            y = jnp.dot(spectrum, table[...], preferred_element_type=F32)
+            rows[step % 2, h * HALF : (h + 1) * HALF] = y.astype(BF).reshape(HALF, REFS, LAGS)
         put(step).start()
         return carry
 
@@ -357,7 +362,6 @@
             pltpu.VMEM((REFS * ROWS, 128), F32),
             pltpu.VMEM((ROWS, REFS, 128), BF),
             pltpu.VMEM((GROUP, ROWS, 128), F32),
-            pltpu.VMEM((GROUP * REFS, SEG), BF),
             pltpu.VMEM((2, GROUP, REFS, LAGS), BF),
             pltpu.SemaphoreType.DMA((3,)),
             pltpu.SemaphoreType.DMA((2,)),

time: 69.6 us -> 63.4 us (0.911)
  Pallas kernels: 68 us -> 61.8 us
    pallas_call x1, Pallas kernels: 24.5 us -> 18.2 us  [correlate(): pl.pallas_call(correlate_kernel, name='correlate', in_specs=[hbm] * 3 + [...]
where the time goes in v3:
time: 63.4 us; the launch traced here: 63.3 us
  Pallas kernels  61.8 us (97%)
  other arithmetic  0.75 us (1%)
  between operations  0.72 us (1%)
    pallas_call x1, Pallas kernels, exchange(): pl.pallas_call(exchange_kernel, name='exchange', in_specs=[vmem] * 3, out...  38.4 us
    pallas_call x1, Pallas kernels, correlate(): pl.pallas_call(correlate_kernel, name='correlate', in_specs=[hbm] * 3 + [...  18.2 us
    pallas_call x1, Pallas kernels, spectra(): pl.pallas_call(spectra_kernel, name='spectra', in_specs=[hbm] * 3, out_sp...  5.13 us

profile of v3, /device:TPU:1, one launch (start us, length us, event | category | flops | bytes accessed | tf_op | source)
XLA Modules:
  0.0 63.3 jit_solution(8856657170096152696)
XLA Ops:
  0.7 0.8 %pad_add_fusion.ints_in = s32[128]{0:T(128)S(1)} fusion(s32[59]{0:T(128)S(1)} %broadcast_in_dim.3, s32[1]{0:T(128)S(6)} %copy.10, s32[4]{0:T(128)} %param.10, s32[64]{0:T(128)} %param.11), kind=kLoop, calls=%fused_computation | loop fusion | flops 384 | bytes 1024 | tf_op jit(solution)/shard_map/concatenate | solution.py:90
  1.4 0.0 copy-start
  1.4 0.0 copy-start.1
  1.4 0.0 copy-start.2
  1.4 0.0 copy-start.3
  1.4 5.1 %spectra.1 = (bf16[128,32,128]{2,1,0:T(8,128)(2,1)S(1)}, bf16[1,32,128]{2,1,0:T(8,128)(2,1)S(1)}, bf16[64,32,128]{2,1,0:T(8,128)(2,1)S(1)}) custom-call(s32[128]{0:T(128)S(1)} %pad_add_fusion.ints_in, bf16[128,4096]{1,0:T(8,128)(2,1)} %raw.1, bf16[1024,1024]{1,0:T(8,128)(2,1)} %constant.6.clone.table_in), custom_call_target="tpu_custom_call" | custom-call | tf_op jit(solution)/shard_map/spectra/pallas_call | solution.py:91
  6.6 38.4 %exchange.1 = (bf16[160,32,128]{2,1,0:T(8,128)(2,1)S(1)}, bf16[256,32,128]{2,1,0:T(8,128)(2,1)S(1)}, bf16[64,32,128]{2,1,0:T(8,128)(2,1)S(1)}) custom-call(bf16[128,32,128]{2,1,0:T(8,128)(2,1)S(1)} %get-tuple-element.11.white, bf16[1,32,128]{2,1,0:T(8,128)(2,1)S(1)} %get-tuple-element.12.export, bf16[64,32,128]{2,1,0:T(8,128)(2,1)S(1)} %get-tuple-element.13.picked), custom_call_target="tpu_custom_call" | custom-call | tf_op jit(solution)/shard_map/exchange/pallas_call | solution.py:246
  45.0 0.0 copy-done
  45.0 0.0 copy-done.1
  45.0 0.0 copy-done.2
  45.0 0.0 copy-done.3
  45.0 18.2 %correlate.1 = bf16[128,64,512]{2,1,0:T(8,128)(2,1)} custom-call(s32[8,128]{1,0:T(8,128)S(1)} %bitcast.3, s32[2,128]{1,0:T(2,128)S(1)} %bitcast.4, s32[2,128]{1,0:T(2,128)S(1)} %bitcast.5, bf16[160,32,128]{2,1,0:T(8,128)(2,1)S(1)} %get-tuple-element.14.ext, bf16[256,32,128]{2,1,0:T(8,128)(2,1)S(1)} %get-tuple-element.15.pool, ...), custom_call_target="tpu_custom_call" | custom-call | tf_op jit(solution)/shard_map/correlate/pallas_call | solution.py:352
  (1 shorter events, 0.0 us)
Async XLA Ops:
  1.4 43.6 %copy-start = (bf16[1024,512]{1,0:T(8,128)(2,1)S(1)}, bf16[1024,512]{1,0:T(8,128)(2,1)}, u32[]{:S(2)}) copy-start(bf16[1024,512]{1,0:T(8,128)(2,1)} %constant.7.clone.table) | copy-start | bytes 3145732
  1.4 43.6 %copy-start.1 = (s32[128,8]{0,1:T(8,128)S(1)}, s32[128,8]{0,1:T(8,128)}, u32[]{:S(2)}) copy-start(s32[128,8]{0,1:T(8,128)} %param.12) | copy-start | bytes 12292
  1.4 43.6 %copy-start.2 = (s32[128,2]{0,1:T(2,128)S(1)}, s32[128,2]{0,1:T(2,128)}, u32[]{:S(2)}) copy-start(s32[128,2]{0,1:T(2,128)} %param.13) | copy-start | bytes 3076
  1.4 43.6 %copy-start.3 = (s32[128,2]{0,1:T(2,128)S(1)}, s32[128,2]{0,1:T(2,128)}, u32[]{:S(2)}) copy-start(s32[128,2]{0,1:T(2,128)} %param.14) | copy-start | bytes 3076

commit v4 on v3

--- a/solution.py
+++ b/solution.py
@@ -20,6 +20,8 @@
 ROWS = SEGS * SEG // 128
 GROUP = 16
 HALF = 8
+FAR_RING4 = (2, 1, 3)
+FAR_RING8 = (4, 3, 5, 2, 6, 1, 7)
 MESH = pl.DeviceIdType.MESH
 BF = jnp.bfloat16
 F32 = jnp.float32
@@ -55,9 +57,17 @@
     for s in range(SEGS):
         begin = ints[REFS + s]
         lead = pl.multiple_of((begin // 128) * 128, 128)
-        window = samples[:, pl.ds(lead, SEG + 128)].astype(F32)
-        cut = pltpu.roll(window, (SEG + 128) - (begin - lead), 1)[:, :SEG]
-        seg[s * CH : (s + 1) * CH, :] = cut.astype(BF)
+        offset = begin - lead
+        turned = [
+            pltpu.roll(
+                samples[:, pl.ds(lead + j * 128, 128)].astype(F32), (128 - offset) % 128, 1
+            )
+            for j in range(SEG // 128 + 1)
+        ]
+        here = lax.broadcasted_iota(jnp.int32, (CH, 128), 1) < 128 - offset
+        for j in range(SEG // 128):
+            cut = jnp.where(here, turned[j], turned[j + 1]).astype(BF)
+            seg[s * CH : (s + 1) * CH, j * 128 : (j + 1) * 128] = cut
     loads[2].wait()
     for s in range(SEGS):
         spectrum = jnp.dot(
@@ -159,13 +169,14 @@
         sent.extend(copies)
 
     partner = (1 - k, chan)
-    whole = pool.reshape(2, NZ, NA, NB, ROWS, 128)
+    whole = pool.at[pl.ds(0, 2 * CH)].reshape(2, NZ, NA, NB, ROWS, 128)
 
     pool[pl.ds(k * CH + own, 1)] = export[...]
+    pool[pl.ds(2 * CH, 1)] = jnp.zeros((1, ROWS, 128), BF)
     pl.semaphore_wait(barrier, len(peers))
     core = start(picked.at[pl.ds((1 - k) * (REFS // 2), REFS // 2)], core_in, partner)
     mine = pool.at[pl.ds(k * CH + own, 1)]
-    pool_z = [start(export, mine, (k, c)) for c in z_peer]
+    pool_z = [start(export, mine, (k, z_peer[j - 1])) for j in FAR_RING8]
     halos = [
         start(white.at[pl.ds(CH - HALO, HALO)], ext.at[pl.ds(0, HALO)], (k, up)),
         start(white.at[pl.ds(0, HALO)], ext.at[pl.ds(HALO + CH, HALO)], (k, down)),
@@ -175,12 +186,12 @@
     half[...] = picked[pl.ds(k * (REFS // 2), REFS // 2)] + core_in[...]
     a_rs = [
         start(half.at[pl.ds(((a + j) % NA) * 8, 8)], a_in.at[j - 1], (k, a_peer[j - 1]))
-        for j in range(1, NA)
+        for j in FAR_RING4
     ]
 
     arrive(pool_z)
     column = whole.at[k, :, a, b]
-    pool_a = [start(column, column, (k, c)) for c in a_peer]
+    pool_a = [start(column, column, (k, a_peer[j - 1])) for j in FAR_RING4]
     pool_c = [start(column, column, partner)]
     ext[HALO : HALO + CH] = white[...]
 
@@ -188,12 +199,12 @@
     a_sum[...] = half[pl.ds(a * 8, 8)] + a_in[0] + a_in[1] + a_in[2]
     b_rs = [
         start(a_sum.at[pl.ds(((b + j) % NB) * 2, 2)], b_in.at[j - 1], (k, b_peer[j - 1]))
-        for j in range(1, NB)
+        for j in FAR_RING4
     ]
 
     arrive(b_rs)
     b_sum[...] = a_sum[pl.ds(b * 2, 2)] + b_in[0] + b_in[1] + b_in[2]
-    z_rs = [start(b_sum, z_in.at[j - 1], (k, z_peer[j - 1])) for j in range(1, NZ)]
+    z_rs = [start(b_sum, z_in.at[j - 1], (k, z_peer[j - 1])) for j in FAR_RING8]
 
     arrive(pool_a)
     plane = whole.at[k, :, :, b]
@@ -209,7 +220,7 @@
     lead = k * (REFS // 2) + a * 8
     pair = refs.at[pl.ds(lead + b * 2, 2)]
     refs[pl.ds(lead + b * 2, 2)] = total
-    refs_b = [start(pair, pair, (k, c)) for c in b_peer]
+    refs_b = [start(pair, pair, (k, b_peer[j - 1])) for j in FAR_RING4]
 
     arrive(pool_b)
     low = whole.at[k, pl.ds(0, NZ // 2), :, (b + NB - 1) % NB]
@@ -218,7 +229,7 @@
 
     arrive(refs_b)
     eight = refs.at[pl.ds(lead, 8)]
-    refs_a = [start(eight, eight, (k, c)) for c in a_peer]
+    refs_a = [start(eight, eight, (k, a_peer[j - 1])) for j in FAR_RING4]
     refs_c = [start(eight, eight, partner)]
     for c in ((b + NB - 1) % NB, (b + 1) % NB):
         got = whole.at[k, :, :, c]
@@ -228,8 +239,8 @@
     got = whole.at[k, :, :, (b + 2) % NB]
     pool_c.append(start(got, got, partner))
 
-    for j in range(1, NA):
-        arrive([refs_a[j - 1]])
+    for copy, j in zip(refs_a, FAR_RING4):
+        arrive([copy])
         got = refs.at[pl.ds(k * (REFS // 2) + ((a + NA - j) % NA) * 8, 8)]
         refs_c.append(start(got, got, partner))
 
@@ -250,7 +261,7 @@
         out_specs=[vmem] * 3,
         out_shape=[
             jax.ShapeDtypeStruct((CH + 2 * HALO, ROWS, 128), BF),
-            jax.ShapeDtypeStruct((2 * CH, ROWS, 128), BF),
+            jax.ShapeDtypeStruct((2 * CH + 1, ROWS, 128), BF),
             jax.ShapeDtypeStruct((REFS, ROWS, 128), BF),
         ],
         scratch_shapes=[
@@ -288,14 +299,20 @@
 
 
 def correlate_kernel(
-    near_in, cross_in, mask_in, ext, pool, refs, table, out,
-    near, cross, mask, wide, right, left, rows, load, store,
+    near, cross, mask, ext, pool, refs, table, out,
+    index_rows, share_row, index, shares, wide, right, left, rows, load, store,
 ):
     base = (lax.axis_index("fibre") * (NZ * NA * NB) + lax.axis_index("chan")) * CH
+    index_rows[0:NN, :] = near[...] - (base - HALO)
+    p = cross[...]
+    swapped = (p & ~15) | ((p & 3) << 2) | ((p >> 2) & 3)
+    index_rows[NN : NN + XN, :] = jnp.where(mask[...] == 1, jnp.where(p < CH, p, swapped), 2 * CH)
+    index_rows[NN + XN :, :] = jnp.zeros((16 - NN - XN, CH), jnp.int32)
+    count = (1.0 + NN) + jnp.sum(mask[...].astype(F32), 0, keepdims=True)
+    share_row[...] = 1.0 / count
     loads = [
-        pltpu.make_async_copy(near_in, near, load.at[0]),
-        pltpu.make_async_copy(cross_in, cross, load.at[1]),
-        pltpu.make_async_copy(mask_in, mask, load.at[2]),
+        pltpu.make_async_copy(index_rows, index, load.at[0]),
+        pltpu.make_async_copy(share_row, shares, load.at[1]),
     ]
     for copy in loads:
         copy.start()
@@ -316,16 +333,10 @@
             chan = step * GROUP + c
             total = ext[HALO + chan].astype(F32)
             for n in range(NN):
-                total = total + ext[near[n, chan] - base + HALO].astype(F32)
-            links = 0
-            for j in range(XN):
-                p = cross[j, chan]
-                swapped = (p & ~15) | ((p & 3) << 2) | ((p >> 2) & 3)
-                live = mask[j, chan]
-                total = total + pool[jnp.where(p < CH, p, swapped)].astype(F32) * live.astype(F32)
-                links = links + live
-            share = jnp.where(links == 0, 1.0 / 9, jnp.where(links == 1, 0.1, 1.0 / 11)).astype(F32)
-            left[c] = (total * share).astype(BF).astype(F32)
+                total = total + ext[index[n, chan]].astype(F32)
+            for n in range(NN, NN + XN):
+                total = total + pool[index[n, chan]].astype(F32)
+            left[c] = (total * shares[0, chan]).astype(BF).astype(F32)
 
         @pl.when(step >= 2)
         def _():
@@ -352,18 +363,19 @@
     return pl.pallas_call(
         correlate_kernel,
         name="correlate",
-        in_specs=[hbm] * 3 + [vmem] * 4,
+        in_specs=[vmem] * 7,
         out_specs=hbm,
         out_shape=jax.ShapeDtypeStruct((CH, REFS, LAGS), BF),
         scratch_shapes=[
-            pltpu.SMEM((NN, CH), jnp.int32),
-            pltpu.SMEM((XN, CH), jnp.int32),
-            pltpu.SMEM((XN, CH), jnp.int32),
+            pltpu.VMEM((16, CH), jnp.int32),
+            pltpu.VMEM((1, CH), F32),
+            pltpu.SMEM((16, CH), jnp.int32),
+            pltpu.SMEM((1, CH), F32),
             pltpu.VMEM((REFS * ROWS, 128), F32),
             pltpu.VMEM((ROWS, REFS, 128), BF),
             pltpu.VMEM((GROUP, ROWS, 128), F32),
             pltpu.VMEM((2, GROUP, REFS, LAGS), BF),
-            pltpu.SemaphoreType.DMA((3,)),
+            pltpu.SemaphoreType.DMA((2,)),
             pltpu.SemaphoreType.DMA((2,)),
         ],
         compiler_params=pltpu.CompilerParams(vmem_limit_bytes=24 << 20),

time: 63.4 us -> 61.3 us (0.967)
  Pallas kernels: 61.8 us -> 59.7 us
    pallas_call x1, Pallas kernels: 38.4 us -> 37.3 us  [exchange(): pl.pallas_call(exchange_kernel, name='exchange', in_specs=[vmem] * 3, out...]
    pallas_call x1, Pallas kernels: 18.2 us -> 17.3 us  [correlate(): pl.pallas_call(correlate_kernel, name='correlate', in_specs=[vmem] * 7, o...]
where the time goes in v4:
time: 61.3 us; the launch traced here: 61.2 us
  Pallas kernels  59.7 us (97%)
  other arithmetic  0.75 us (1%)
  between operations  0.72 us (1%)
    pallas_call x1, Pallas kernels, exchange(): pl.pallas_call(exchange_kernel, name='exchange', in_specs=[vmem] * 3, out...  37.3 us
    pallas_call x1, Pallas kernels, correlate(): pl.pallas_call(correlate_kernel, name='correlate', in_specs=[vmem] * 7, o...  17.3 us
    pallas_call x1, Pallas kernels, spectra(): pl.pallas_call(spectra_kernel, name='spectra', in_specs=[hbm] * 3, out_sp...  5.07 us

profile of v4, /device:TPU:1, one launch (start us, length us, event | category | flops | bytes accessed | tf_op | source)
XLA Modules:
  0.0 61.2 jit_solution(17165974960489695562)
XLA Ops:
  0.7 0.8 %pad_add_fusion.ints_in = s32[128]{0:T(128)S(1)} fusion(s32[59]{0:T(128)S(1)} %broadcast_in_dim.3, s32[1]{0:T(128)S(6)} %copy.10, s32[4]{0:T(128)} %param.10, s32[64]{0:T(128)} %param.11), kind=kLoop, calls=%fused_computation | loop fusion | flops 384 | bytes 1024 | tf_op jit(solution)/shard_map/concatenate | solution.py:100
  1.4 0.0 copy-start
  1.4 0.0 copy-start.1
  1.4 0.0 copy-start.2
  1.4 0.0 copy-start.3
  1.4 5.1 %spectra.1 = (bf16[128,32,128]{2,1,0:T(8,128)(2,1)S(1)}, bf16[1,32,128]{2,1,0:T(8,128)(2,1)S(1)}, bf16[64,32,128]{2,1,0:T(8,128)(2,1)S(1)}) custom-call(s32[128]{0:T(128)S(1)} %pad_add_fusion.ints_in, bf16[128,4096]{1,0:T(8,128)(2,1)} %raw.1, bf16[1024,1024]{1,0:T(8,128)(2,1)} %constant.6.clone.table_in), custom_call_target="tpu_custom_call" | custom-call | tf_op jit(solution)/shard_map/spectra/pallas_call | solution.py:101
  6.5 37.3 %exchange.1 = (bf16[160,32,128]{2,1,0:T(8,128)(2,1)S(1)}, bf16[257,32,128]{2,1,0:T(8,128)(2,1)S(1)}, bf16[64,32,128]{2,1,0:T(8,128)(2,1)S(1)}) custom-call(bf16[128,32,128]{2,1,0:T(8,128)(2,1)S(1)} %get-tuple-element.11.white, bf16[1,32,128]{2,1,0:T(8,128)(2,1)S(1)} %get-tuple-element.12.export, bf16[64,32,128]{2,1,0:T(8,128)(2,1)S(1)} %get-tuple-element.13.picked), custom_call_target="tpu_custom_call" | custom-call | tf_op jit(solution)/shard_map/exchange/pallas_call | solution.py:257
  43.8 0.0 copy-done
  43.8 0.0 copy-done.1
  43.8 0.0 copy-done.2
  43.9 0.0 copy-done.3
  43.9 17.3 %correlate.1 = bf16[128,64,512]{2,1,0:T(8,128)(2,1)} custom-call(s32[8,128]{1,0:T(8,128)S(1)} %bitcast.3, s32[2,128]{1,0:T(2,128)S(1)} %bitcast.4, s32[2,128]{1,0:T(2,128)S(1)} %bitcast.5, bf16[160,32,128]{2,1,0:T(8,128)(2,1)S(1)} %get-tuple-element.14.ext, bf16[257,32,128]{2,1,0:T(8,128)(2,1)S(1)} %get-tuple-element.15.pool, ...), custom_call_target="tpu_custom_call" | custom-call | tf_op jit(solution)/shard_map/correlate/pallas_call | solution.py:363
  (1 shorter events, 0.0 us)
Async XLA Ops:
  1.4 42.4 %copy-start = (bf16[1024,512]{1,0:T(8,128)(2,1)S(1)}, bf16[1024,512]{1,0:T(8,128)(2,1)}, u32[]{:S(2)}) copy-start(bf16[1024,512]{1,0:T(8,128)(2,1)} %constant.7.clone.table) | copy-start | bytes 3145732
  1.4 42.4 %copy-start.1 = (s32[128,8]{0,1:T(8,128)S(1)}, s32[128,8]{0,1:T(8,128)}, u32[]{:S(2)}) copy-start(s32[128,8]{0,1:T(8,128)} %param.12) | copy-start | bytes 12292
  1.4 42.4 %copy-start.2 = (s32[128,2]{0,1:T(2,128)S(1)}, s32[128,2]{0,1:T(2,128)}, u32[]{:S(2)}) copy-start(s32[128,2]{0,1:T(2,128)} %param.13) | copy-start | bytes 3076
  1.4 42.4 %copy-start.3 = (s32[128,2]{0,1:T(2,128)S(1)}, s32[128,2]{0,1:T(2,128)}, u32[]{:S(2)}) copy-start(s32[128,2]{0,1:T(2,128)} %param.14) | copy-start | bytes 3076

commit v5 on v4

--- a/solution.py
+++ b/solution.py
@@ -328,7 +328,7 @@
             rows.at[step % 2], out.at[pl.ds(step * GROUP, GROUP)], store.at[step % 2]
         )
 
-    def body(step, carry):
+    def smooth(step):
         for c in range(GROUP):
             chan = step * GROUP + c
             total = ext[HALO + chan].astype(F32)
@@ -338,6 +338,7 @@
                 total = total + pool[index[n, chan]].astype(F32)
             left[c] = (total * shares[0, chan]).astype(BF).astype(F32)
 
+    def body(step, carry):
         @pl.when(step >= 2)
         def _():
             put(step - 2).wait()
@@ -346,12 +347,14 @@
             jnp.concatenate([products(left, right, c) for c in range(h, h + HALF)], 0)
             for h in range(0, GROUP, HALF)
         ]
+        smooth(jnp.minimum(step + 1, steps - 1))
         for h, spectrum in enumerate(cross_spectra):
             y = jnp.dot(spectrum, table[...], preferred_element_type=F32)
             rows[step % 2, h * HALF : (h + 1) * HALF] = y.astype(BF).reshape(HALF, REFS, LAGS)
         put(step).start()
         return carry
 
+    smooth(0)
     lax.fori_loop(0, steps, body, 0)
     put(steps - 2).wait()
     put(steps - 1).wait()

time: 61.3 us -> 62 us (1.011)
  Pallas kernels: 59.7 us -> 60.4 us
    pallas_call x1, Pallas kernels: 17.3 us -> 18.1 us  [correlate(): pl.pallas_call(correlate_kernel, name='correlate', in_specs=[vmem] * 7, o...]
where the time goes in v5:
time: 62 us; the launch traced here: 61.9 us
  Pallas kernels  60.4 us (97%)
  other arithmetic  0.75 us (1%)
  between operations  0.72 us (1%)
    pallas_call x1, Pallas kernels, exchange(): pl.pallas_call(exchange_kernel, name='exchange', in_specs=[vmem] * 3, out...  37.3 us
    pallas_call x1, Pallas kernels, correlate(): pl.pallas_call(correlate_kernel, name='correlate', in_specs=[vmem] * 7, o...  18.1 us
    pallas_call x1, Pallas kernels, spectra(): pl.pallas_call(spectra_kernel, name='spectra', in_specs=[hbm] * 3, out_sp...  5.07 us

profile of v5, /device:TPU:1, one launch (start us, length us, event | category | flops | bytes accessed | tf_op | source)
XLA Modules:
  0.0 61.9 jit_solution(1359619125103371610)
XLA Ops:
  0.7 0.8 %pad_add_fusion.ints_in = s32[128]{0:T(128)S(1)} fusion(s32[59]{0:T(128)S(1)} %broadcast_in_dim.3, s32[1]{0:T(128)S(6)} %copy.10, s32[4]{0:T(128)} %param.10, s32[64]{0:T(128)} %param.11), kind=kLoop, calls=%fused_computation | loop fusion | flops 384 | bytes 1024 | tf_op jit(solution)/shard_map/concatenate | solution.py:100
  1.4 0.0 copy-start
  1.4 0.0 copy-start.1
  1.4 0.0 copy-start.2
  1.4 0.0 copy-start.3
  1.4 5.1 %spectra.1 = (bf16[128,32,128]{2,1,0:T(8,128)(2,1)S(1)}, bf16[1,32,128]{2,1,0:T(8,128)(2,1)S(1)}, bf16[64,32,128]{2,1,0:T(8,128)(2,1)S(1)}) custom-call(s32[128]{0:T(128)S(1)} %pad_add_fusion.ints_in, bf16[128,4096]{1,0:T(8,128)(2,1)} %raw.1, bf16[1024,1024]{1,0:T(8,128)(2,1)} %constant.6.clone.table_in), custom_call_target="tpu_custom_call" | custom-call | tf_op jit(solution)/shard_map/spectra/pallas_call | solution.py:101
  6.5 37.3 %exchange.1 = (bf16[160,32,128]{2,1,0:T(8,128)(2,1)S(1)}, bf16[257,32,128]{2,1,0:T(8,128)(2,1)S(1)}, bf16[64,32,128]{2,1,0:T(8,128)(2,1)S(1)}) custom-call(bf16[128,32,128]{2,1,0:T(8,128)(2,1)S(1)} %get-tuple-element.11.white, bf16[1,32,128]{2,1,0:T(8,128)(2,1)S(1)} %get-tuple-element.12.export, bf16[64,32,128]{2,1,0:T(8,128)(2,1)S(1)} %get-tuple-element.13.picked), custom_call_target="tpu_custom_call" | custom-call | tf_op jit(solution)/shard_map/exchange/pallas_call | solution.py:257
  43.8 0.0 copy-done
  43.8 0.0 copy-done.1
  43.8 0.0 copy-done.2
  43.9 0.0 copy-done.3
  43.9 18.1 %correlate.1 = bf16[128,64,512]{2,1,0:T(8,128)(2,1)} custom-call(s32[8,128]{1,0:T(8,128)S(1)} %bitcast.3, s32[2,128]{1,0:T(2,128)S(1)} %bitcast.4, s32[2,128]{1,0:T(2,128)S(1)} %bitcast.5, bf16[160,32,128]{2,1,0:T(8,128)(2,1)S(1)} %get-tuple-element.14.ext, bf16[257,32,128]{2,1,0:T(8,128)(2,1)S(1)} %get-tuple-element.15.pool, ...), custom_call_target="tpu_custom_call" | custom-call | tf_op jit(solution)/shard_map/correlate/pallas_call | solution.py:366
  (1 shorter events, 0.0 us)
Async XLA Ops:
  1.4 42.4 %copy-start = (bf16[1024,512]{1,0:T(8,128)(2,1)S(1)}, bf16[1024,512]{1,0:T(8,128)(2,1)}, u32[]{:S(2)}) copy-start(bf16[1024,512]{1,0:T(8,128)(2,1)} %constant.7.clone.table) | copy-start | bytes 3145732
  1.4 42.4 %copy-start.1 = (s32[128,8]{0,1:T(8,128)S(1)}, s32[128,8]{0,1:T(8,128)}, u32[]{:S(2)}) copy-start(s32[128,8]{0,1:T(8,128)} %param.12) | copy-start | bytes 12292
  1.4 42.4 %copy-start.2 = (s32[128,2]{0,1:T(2,128)S(1)}, s32[128,2]{0,1:T(2,128)}, u32[]{:S(2)}) copy-start(s32[128,2]{0,1:T(2,128)} %param.13) | copy-start | bytes 3076
  1.4 42.4 %copy-start.3 = (s32[128,2]{0,1:T(2,128)S(1)}, s32[128,2]{0,1:T(2,128)}, u32[]{:S(2)}) copy-start(s32[128,2]{0,1:T(2,128)} %param.14) | copy-start | bytes 3076
